TPU v7x, 128 devices: a whole 4x4x4 slice. The times are simulated.
128 devices in a mesh: row: 16 (over y, z), col: 8 (over x, core).
Axes of the slice: x: 4, y: 4, z: 4, core: 2. Of those that a mesh axis runs over, the one named last changes fastest.
Arguments:
- noise: float32 [16384, 512], P(('row', 'col')), may hold values from -40 to 40
- data: float32 [16384, 512], P(('col', 'row')), may hold values from -6 to 6
Outputs:
- noise_target: float32 [16384, 512], P(('row', 'col'))
- data_target: float32 [16384, 512], P(('col', 'row'))
- f_potential: float32 [16384], P('row')
- g_potential: float32 [16384], P('col')
All inputs are finite; a program needn't handle non-finite values.
Results may differ from a plain program's by a relative error of at most 0.0003.
Values sent between devices are 32-bit elements; how exact they have to be, the bound alone decides.
No kernel may reach another device: no remote copies, remote signals or barrier semaphores. Data moves between devices by JAX's collectives and lax.ppermute only.
A program may use at most 64 MiB of HBM per device.

v0:
```python
import functools

import jax
import jax.numpy as jnp
from jax import lax
from jax.experimental import pallas as pl
from jax.experimental.pallas import tpu as pltpu
from jax.sharding import Mesh
from jax.sharding import PartitionSpec as P

ALL = ("y", "z", "x", "c")
PAIRS_A = ((0, 1), (2, 3))
PAIRS_B = ((1, 2), (0, 3))
UP = [(i, (i + 1) % 4) for i in range(4)]
DOWN = [(i, (i - 1) % 4) for i in range(4)]
CORES = [(0, 1), (1, 0)]


def place(y, z, x, c):
    return ((y * 4 + z) * 4 + x) * 2 + c


SAME_ROWS = [
    [place(y, z, x, c) for y in pair for x in range(4)]
    for pair in PAIRS_A
    for z in range(4)
    for c in range(2)
]
SAME_COLUMNS = [
    [place(y, z, x, c) for y in pair for z in range(4)]
    for pair in PAIRS_B
    for x in range(4)
    for c in range(2)
]

EPSILON = 32.0
LOG2E = 1.4426950408889634
LN2 = 0.6931471805599453
SCALE = LOG2E / EPSILON
BLOCK = 256
WIDE = 512
CHUNK = 64
VMEM_LIMIT = 32 * 1024 * 1024


def split(v):
    high = v.astype(jnp.bfloat16)
    return high, (v - high.astype(jnp.float32)).astype(jnp.bfloat16)


def dot(a, b, dims):
    return lax.dot_general(a, b, (dims, ((), ())), preferred_element_type=jnp.float32)


def as_column(row):
    return jnp.broadcast_to(row, (128, row.shape[1])).T


def as_row(column):
    return column.T[0:1, :]


def call(
    kernel, arrays, out_shape, scratch=(), flops=0, transcendentals=0, scalars=(), far=(), far_out=0
):
    anywhere = pl.BlockSpec(memory_space=pltpu.HBM)
    vmem = pl.BlockSpec(memory_space=pltpu.VMEM)
    smem = pl.BlockSpec(memory_space=pltpu.SMEM)
    moved = sum(v.size * v.dtype.itemsize for v in (*far, *arrays, *out_shape))
    return pl.pallas_call(
        kernel,
        in_specs=[smem] * len(scalars) + [anywhere] * len(far) + [vmem] * len(arrays),
        out_specs=[anywhere] * far_out + [vmem] * (len(out_shape) - far_out),
        out_shape=[
            pltpu.HBM(v.shape, v.dtype) if k < far_out else v for k, v in enumerate(out_shape)
        ],
        scratch_shapes=scratch,
        cost_estimate=pl.CostEstimate(
            flops=flops, bytes_accessed=moved, transcendentals=transcendentals
        ),
        compiler_params=pltpu.CompilerParams(vmem_limit_bytes=VMEM_LIMIT),
    )(*scalars, *(pltpu.with_memory_space_constraint(v, pltpu.HBM) for v in far), *arrays)


def started(copies):
    for copy in copies:
        copy.start()
    return copies


def matrix_scratch(n, m):
    half = pltpu.VMEM((m // BLOCK, n, BLOCK), jnp.bfloat16)
    return half, half, pltpu.SemaphoreType.DMA((2, m // BLOCK))


def block_copies(j, high_from, low_from, high, low, arrived, first=0):
    return [
        pltpu.make_async_copy(a.at[first + j], b.at[j], arrived.at[side, j])
        for side, (a, b) in enumerate(((high_from, high), (low_from, low)))
    ]


def wait(copies):
    for copy in copies:
        copy.wait()


def span(k, size):
    return pl.ds(pl.multiple_of(k * size, size), size)


def f32(*shape):
    return jax.ShapeDtypeStruct(shape, jnp.float32)


def scores_kernel(*refs):
    slots, xs, ys = refs[0], refs[1:9], refs[9:25]
    xt_out, s_ref, lse_ref, xn_ref, yn_ref = refs[25:30]
    xk, yk, peak, total, x, y, xt, arrived, sent = refs[30:]
    n, m = s_ref.shape
    w = y.shape[1]
    steps = m // WIDE

    def norms(v):
        return as_row(jnp.broadcast_to(jnp.sum(v * v, axis=1, keepdims=True), (128, 128)))

    here = [(x if k < 8 else y).at[span(slots[k], 128)] for k in range(24)]
    copies = started(
        [
            pltpu.make_async_copy(a, b, arrived.at[k])
            for k, (a, b) in enumerate(zip((*xs, *ys), here))
        ]
    )
    wait(copies[:8])

    def place_row_block(k, carry):
        at = span(k, 128)
        v = x[at, :]
        xt[:, at] = v.T
        xn_ref[:, at] = norms(v)
        high, low = split(v * (2.0 * SCALE))
        xk[at, :w] = high
        xk[at, w : 2 * w] = high
        xk[at, 2 * w :] = low
        return carry

    lax.fori_loop(0, 8, place_row_block, 0)
    kept = pltpu.make_async_copy(xt, xt_out, sent)
    kept.start()
    wait(copies[8:])

    def prepare(j):
        for k in range(WIDE // 128):
            at = span(j * (WIDE // 128) + k, 128)
            v = y[at, :]
            yn_ref[:, at] = norms(v)
            high, low = split(v)
            yk[at, :w] = high
            yk[at, w : 2 * w] = low
            yk[at, 2 * w :] = high

    prepare(0)
    peak[...] = jnp.full_like(peak, -jnp.inf)
    total[...] = jnp.zeros_like(total)

    def multiply(j):
        at = span(j, WIDE)
        s_ref[:, at] = dot(xk[...], yk[at, :], ((1,), (1,)))

    def collect(j):
        at = span(j, WIDE)
        shift = SCALE * yn_ref[:, at]
        for i in range(0, n, CHUNK // 2):
            rows = slice(i, i + CHUNK // 2)
            t = s_ref[rows, at] - shift
            old = peak[rows, :]
            lanes = [t[:, k : k + 128] for k in range(0, WIDE, 128)]
            new = functools.reduce(jnp.maximum, lanes, old)
            part = sum(jnp.exp2(v - new) for v in lanes)
            total[rows, :] = total[rows, :] * jnp.exp2(old - new) + part
            peak[rows, :] = new

    multiply(0)
    prepare(1)

    def step(j, carry):
        multiply(j)
        collect(j - 1)
        prepare(jnp.minimum(j + 1, steps - 1))
        return carry

    lax.fori_loop(1, steps, step, 0)
    collect(steps - 1)
    top = jnp.max(peak[...], axis=1, keepdims=True)
    sums = jnp.sum(total[...] * jnp.exp2(peak[...] - top), axis=1, keepdims=True)
    lse_ref[...] = as_row(jnp.broadcast_to(top + jnp.log2(sums), peak.shape))
    kept.wait()


def scores_of(slots, xs, ys):
    n, m, w = 8 * 128, 16 * 128, xs[0].shape[1]
    return call(
        scores_kernel,
        (),
        (f32(w, n), f32(n, m), f32(1, n), f32(1, n), f32(1, m)),
        (
            pltpu.VMEM((n, 3 * w), jnp.bfloat16),
            pltpu.VMEM((m, 3 * w), jnp.bfloat16),
            pltpu.VMEM((n, 128), jnp.float32),
            pltpu.VMEM((n, 128), jnp.float32),
            pltpu.VMEM((n, w), jnp.float32),
            pltpu.VMEM((m, w), jnp.float32),
            pltpu.VMEM((w, n), jnp.float32),
            pltpu.SemaphoreType.DMA((24,)),
            pltpu.SemaphoreType.DMA,
        ),
        flops=6 * n * m * w,
        transcendentals=n * m,
        scalars=(slots,),
        far=(*xs, *ys),
        far_out=1,
    )


def negative_lse(parts):
    top = jnp.max(parts, axis=0, keepdims=True)
    return -(top + jnp.log2(jnp.sum(jnp.exp2(parts - top), axis=0, keepdims=True)))


def columns_kernel(
    s_ref, parts_ref, high_out, low_out, top_ref, lse_ref, a_ref, a_col, qh_ref, ql_ref, sent
):
    n, m = s_ref.shape
    a = negative_lse(parts_ref[...])
    a_ref[...] = a
    a_col[...] = as_column(a)

    def shifted(i, at):
        a = a_col[i : i + CHUNK, :]
        return s_ref[i : i + CHUNK, at] + jnp.concatenate([a] * (BLOCK // 128), axis=1)

    def folded(v, op):
        return op(v.reshape(CHUNK // 8, 8, BLOCK), axis=0)

    def step(j, carry):
        at = span(j, BLOCK)
        top = jnp.full((8, BLOCK), -jnp.inf, jnp.float32)
        for i in range(0, n, CHUNK):
            top = jnp.maximum(top, folded(shifted(i, at), jnp.max))
        top = jnp.max(top, axis=0, keepdims=True)
        total = jnp.zeros((8, BLOCK), jnp.float32)
        for i in range(0, n, CHUNK):
            q = jnp.exp2(shifted(i, at) - top)
            total = total + folded(q, jnp.sum)
            qh_ref[j, i : i + CHUNK, :], ql_ref[j, i : i + CHUNK, :] = split(q)
        top_ref[:, at] = top
        lse_ref[:, at] = top + jnp.log2(jnp.sum(total, axis=0, keepdims=True))
        started(kept(j))
        return carry

    def kept(j):
        return [
            pltpu.make_async_copy(a.at[j], b.at[j], sent.at[side, j])
            for side, (a, b) in enumerate(((qh_ref, high_out), (ql_ref, low_out)))
        ]

    lax.fori_loop(0, m // BLOCK, step, 0)
    for j in range(m // BLOCK):
        wait(kept(j))


def columns_of(s, parts):
    n, m = s.shape
    half = jax.ShapeDtypeStruct((m // BLOCK, n, BLOCK), jnp.bfloat16)
    return call(
        columns_kernel,
        (s, parts),
        (half, half, f32(1, m), f32(1, m), f32(1, n)),
        (
            pltpu.VMEM((n, 128), jnp.float32),
            *matrix_scratch(n, m),
        ),
        flops=4 * n * m,
        transcendentals=n * m,
        far_out=2,
    )


def joint(high, low):
    return high.astype(jnp.float32) + low.astype(jnp.float32)


def add_weighted(total, high, low, weights):
    for i in range(0, total.shape[0], CHUNK):
        rows = slice(i, i + CHUNK)
        p = joint(high[rows, :], low[rows, :]) * weights
        total[rows, :] += p[:, :128] + p[:, 128:]


def lane_sums(total):
    return as_row(jnp.broadcast_to(jnp.sum(total[...], axis=1, keepdims=True), total.shape))


def rows_kernel(
    high, low, top_ref, parts_ref, sum_ref, t_ref, b_ref, total, qh_ref, ql_ref, arrived
):
    halves = (high, low, qh_ref, ql_ref, arrived)
    steps = qh_ref.shape[0]
    for j in range(steps):
        started(block_copies(j, *halves))
    b = negative_lse(parts_ref[...])
    b_ref[...] = b
    t_ref[...] = jnp.exp2(top_ref[...] + b)
    total[...] = jnp.zeros_like(total)

    def step(j, carry):
        wait(block_copies(j, *halves))
        add_weighted(total, qh_ref.at[j], ql_ref.at[j], t_ref[:, span(j, BLOCK)])
        return carry

    lax.fori_loop(0, steps, step, 0)
    sum_ref[...] = lane_sums(total)


def row_sums(qh, ql, top, parts):
    n, m = qh.shape[1], qh.shape[0] * BLOCK
    return call(
        rows_kernel,
        (top, parts),
        (f32(1, n), f32(1, m), f32(1, m)),
        (pltpu.VMEM((n, 128), jnp.float32), *matrix_scratch(n, m)),
        flops=4 * n * m,
        far=(qh, ql),
    )


def column_sums_kernel(high, low, parts_ref, t_ref, sum_ref, r_ref, inv, qh_ref, ql_ref, arrived):
    halves = (high, low, qh_ref, ql_ref, arrived)
    steps = qh_ref.shape[0]
    for j in range(steps):
        started(block_copies(j, *halves))
    n = inv.shape[0]
    r = jnp.sum(parts_ref[...], axis=0, keepdims=True)
    r_ref[...] = r
    inv[...] = as_column(1.0 / r)

    def step(j, carry):
        wait(block_copies(j, *halves))
        total = jnp.zeros((8, BLOCK), jnp.float32)
        for i in range(0, n, CHUNK):
            rows = slice(i, i + CHUNK)
            scale = jnp.concatenate([inv[rows, :]] * (BLOCK // 128), axis=1)
            q = joint(qh_ref[j, rows, :], ql_ref[j, rows, :]) * scale
            total = total + jnp.sum(q.reshape(CHUNK // 8, 8, BLOCK), axis=0)
        at = span(j, BLOCK)
        sum_ref[:, at] = jnp.sum(total, axis=0, keepdims=True) * t_ref[:, at]
        return carry

    lax.fori_loop(0, steps, step, 0)


def column_sums(qh, ql, parts, t):
    n, m = qh.shape[1], qh.shape[0] * BLOCK
    return call(
        column_sums_kernel,
        (parts, t),
        (f32(1, m), f32(1, n)),
        (pltpu.VMEM((n, 128), jnp.float32), *matrix_scratch(n, m)),
        flops=4 * n * m,
        far=(qh, ql),
    )


def data_kernel(seats, high_from, low_from, xt_from, t_ref, r_ref, *refs):
    outs, (xt, xt_ref, come, qh_ref, ql_ref, arrived, done) = refs[:8], refs[8:]
    w = xt_ref.shape[0]
    steps = qh_ref.shape[0]
    first = pltpu.make_async_copy(xt_from, xt_ref, come)
    first.start()
    halves = (high_from, low_from, qh_ref, ql_ref, arrived, seats[0] * steps)
    for j in range(steps):
        started(block_copies(j, *halves))
    first.wait()
    high, low = split(xt_ref[...] * (1.0 / r_ref[...]))
    n = xt_ref.shape[1]
    xt[:, :n] = high
    xt[:, n : 2 * n] = low
    xt[:, 2 * n :] = high
    inner = ((1,), (0,))

    def step(j, carry):
        wait(block_copies(2 * j, *halves))
        wait(block_copies(2 * j + 1, *halves))
        scale = t_ref[:, span(seats[0] * (steps // 2) + j, 2 * BLOCK)]
        high = jnp.concatenate([qh_ref[2 * j], qh_ref[2 * j + 1]], axis=1)
        low = jnp.concatenate([ql_ref[2 * j], ql_ref[2 * j + 1]], axis=1)
        part = dot(xt[...], jnp.concatenate([high, high, low], axis=0), inner)
        part = (part * scale).T
        for k in range(2 * BLOCK // 128):
            done[seats[1 + j * (2 * BLOCK // 128) + k]] = part[k * 128 : (k + 1) * 128]
        return carry

    lax.fori_loop(0, steps // 2, step, 0)
    for k in range(8):
        outs[k][...] = done[k]


def data_part_of(core, seats, qh, ql, t, r, xt):
    n, m = qh.shape[1], qh.shape[0] * BLOCK
    w = xt.shape[0]
    return call(
        data_kernel,
        (t, r),
        [f32(128, w)] * 8,
        (
            pltpu.VMEM((w, 3 * n), jnp.bfloat16),
            pltpu.VMEM((w, n), jnp.float32),
            pltpu.SemaphoreType.DMA,
            *matrix_scratch(n, m // 2),
            pltpu.VMEM((8, 128, w), jnp.float32),
        ),
        flops=3 * n * m * w,
        far=(qh, ql, xt),
        scalars=(jnp.concatenate([core.reshape(1).astype(jnp.int32), seats]),),
    )


def noise_kernel(seats, high_from, low_from, *refs):
    ys, (parts_ref, t_ref), outs = refs[:16], refs[16:18], refs[18:26]
    c_ref, total, acc, yk, scale, line, y_ref, come, qh_ref, ql_ref, arrived = refs[26:]
    w = y_ref.shape[1]
    moves = started(
        [
            pltpu.make_async_copy(v, y_ref.at[span(seats[8 + k], 128)], come.at[k])
            for k, v in enumerate(ys)
        ]
    )
    halves = (high_from, low_from, qh_ref, ql_ref, arrived)
    steps = qh_ref.shape[0]
    for j in range(steps):
        started(block_copies(j, *halves))
    c = jnp.sum(parts_ref[...], axis=0, keepdims=True)
    c_ref[...] = c
    scale[...] = t_ref[...] / c
    total[...] = jnp.zeros_like(total)
    acc[...] = jnp.zeros_like(acc)
    inner = ((1,), (0,))
    wait(moves)
    depth = steps // 2 * BLOCK

    def scaled(j, carry):
        at = span(j, BLOCK)
        column = jnp.concatenate([as_column(scale[:, at])] * (w // 128), axis=1)
        yh, yl = split(y_ref[at, :] * column)
        half, k = j // (steps // 2), j % (steps // 2)
        yk[half, span(k, BLOCK), :] = yh
        yk[half, pl.ds(pl.multiple_of(depth + k * BLOCK, BLOCK), BLOCK), :] = yl
        yk[half, pl.ds(pl.multiple_of(2 * depth + k * BLOCK, BLOCK), BLOCK), :] = yh
        return carry

    lax.fori_loop(0, steps, scaled, 0)
    parts = acc.shape[0] // BLOCK

    def step(i, carry):
        half, rows = i // parts, span(i % parts, BLOCK)
        blocks = [half * (steps // 2) + k for k in range(steps // 2)]

        @pl.when(i % parts == 0)
        def _():
            for j in blocks:
                wait(block_copies(j, *halves))

        high = [qh_ref[j, rows, :] for j in blocks]
        low = [ql_ref[j, rows, :] for j in blocks]
        acc[rows, :] += dot(jnp.concatenate(high + high + low, axis=1), yk[half], inner)
        for j, a, b in zip(blocks, high, low):
            p = joint(a, b) * scale[:, span(j, BLOCK)]
            total[rows, :] += p[:, :128] + p[:, 128:]
        return carry

    lax.fori_loop(0, 2 * parts, step, 0)
    line[...] = lane_sums(total)
    for k in range(8):
        at = span(seats[k], 128)
        outs[k][:128, :] = acc[at, :]
        sums = jnp.concatenate([line[:, at]] * (w // 128), axis=1)
        outs[k][128:, :] = jnp.broadcast_to(sums, (8, w))


def noise_part_of(seats, qh, ql, parts, t, ys):
    n, m = qh.shape[1], qh.shape[0] * BLOCK
    w = ys[0].shape[1]
    out = call(
        noise_kernel,
        (parts, t),
        [f32(136, w)] * 8 + [f32(1, m)],
        (
            pltpu.VMEM((n, 128), jnp.float32),
            pltpu.VMEM((n, w), jnp.float32),
            pltpu.VMEM((2, 3 * m // 2, w), jnp.bfloat16),
            pltpu.VMEM((1, m), jnp.float32),
            pltpu.VMEM((1, n), jnp.float32),
            pltpu.VMEM((m, w), jnp.float32),
            pltpu.SemaphoreType.DMA((16,)),
            *matrix_scratch(n, m),
        ),
        flops=6 * n * m * w,
        far=(qh, ql, *ys),
        scalars=(seats,),
    )
    return out[:8], out[8]


def pairs(groups):
    return [p for a, b in groups for p in ((a, b), (b, a))]


def gathered(line, groups):
    n, size = line.shape[1], len(groups[0])
    mine = jnp.broadcast_to(line.reshape(1, n // 128, 128), (size, n // 128, 128))
    parts = lax.all_to_all(mine, ALL, 0, 0, axis_index_groups=groups, tiled=True)
    return parts.reshape(size, n)


def spread(own, ring, pair):
    across = pairs(pair)
    below = lax.ppermute(own, ring, UP)
    above = lax.ppermute(own, ring, DOWN)
    over = lax.ppermute(own, "y", across)
    far = lax.ppermute(below, ring, UP)
    over_below = lax.ppermute(over, ring, UP)
    over_above = lax.ppermute(over, ring, DOWN)
    over_far = lax.ppermute(far, "y", across)
    return [own, below, above, over, far, over_below, over_above, over_far]


def sum_to_owner(parts, ring, pair):
    own, up, far, down, over, over_up, over_far, over_down = parts
    across = pairs(pair)
    far = far + lax.ppermute(over_far, "y", across)
    over = over + lax.ppermute(over_up, ring, UP) + lax.ppermute(over_down, ring, DOWN)
    up = up + lax.ppermute(far, ring, UP)
    down = lax.ppermute(down, ring, DOWN)
    return own + down + lax.ppermute(over, "y", across) + lax.ppermute(up, ring, UP)


def shards(noise, data):
    iy, iz, ix, ic = (lax.axis_index(name) for name in ALL)
    row_y, col_y = iy % 2, iy // 2

    xs = spread(noise, "x", PAIRS_A)
    ys = spread(data, "z", PAIRS_B)
    ys = ys + [lax.ppermute(v, "c", CORES) for v in ys]

    hops = ((0, 0), (0, 3), (0, 1), (1, 0), (0, 2), (1, 3), (1, 1), (1, 2))
    row_slots = [(row_y ^ dy) * 4 + (ix + d) % 4 for dy, d in hops]
    col_slots = [(col_y ^ dy) * 4 + (iz + d) % 4 for dy, d in hops]
    slots = jnp.stack(
        row_slots + [ic * 8 + k for k in col_slots] + [(1 - ic) * 8 + k for k in col_slots]
    ).astype(jnp.int32)
    kk = jnp.arange(16, dtype=jnp.int32)
    row_order = ((kk[:8] // 4) ^ row_y) * 4 + (ix + kk[:8]) % 4
    col_seats = ((kk // 4 % 2) ^ col_y) * 4 + (kk - iz) % 4

    xt, s, row_lse, xn, yn = scores_of(slots, xs, ys)
    qh, ql, top, col_lse, a = columns_of(s, gathered(row_lse, SAME_ROWS))
    other = lax.ppermute(col_lse, "c", CORES)
    peak = jnp.maximum(col_lse, other)
    col_lse = peak + jnp.log2(1.0 + jnp.exp2(jnp.minimum(col_lse, other) - peak))
    row_part, t, b = row_sums(qh, ql, top, gathered(col_lse, SAME_COLUMNS))
    col_part, r = column_sums(qh, ql, gathered(row_part, SAME_ROWS), t)
    col_part = col_part + lax.ppermute(col_part, "c", CORES)
    to_other = data_part_of(1 - ic, col_seats, qh, ql, t, r, xt)
    to_own = data_part_of(ic, col_seats, qh, ql, t, r, xt)
    shares = [v + lax.ppermute(u, "c", CORES) for u, v in zip(to_other, to_own)]
    col_part, shares = lax.optimization_barrier((col_part, shares))
    col_parts = gathered(col_part, SAME_COLUMNS)
    data_sum = sum_to_owner(shares, "z", PAIRS_B)
    noise_part, c = noise_part_of(
        jnp.concatenate([row_order, slots[8:]]), qh, ql, col_parts, t, ys
    )
    noise_sum = sum_to_owner(noise_part, "x", PAIRS_A)
    noise_target = noise_sum[:128] / noise_sum[128, :128][:, None]
    mine = lax.dynamic_slice(c, (0, (ic * 8 + col_y * 4 + iz) * 128), (1, 128))
    data_target = data_sum / mine.reshape(128, 1)

    f = (xn + (LN2 * EPSILON) * (a - jnp.log2(r))).reshape(2, 4, 128)
    f_mine = lax.dynamic_index_in_dim(f, row_y, 0, keepdims=False)
    f_other = lax.ppermute(f_mine, "c", CORES)
    f_both = jnp.where(ic == 0, jnp.stack([f_mine, f_other], 1), jnp.stack([f_other, f_mine], 1))
    g = (yn + (LN2 * EPSILON) * (b - jnp.log2(c))).reshape(2, 2, 4, 128)
    g_mine = lax.dynamic_index_in_dim(g, ic, 0, keepdims=False)
    g_other = lax.ppermute(g_mine, "y", pairs(PAIRS_A))
    outer = (iy == 0) | (iy == 3)
    g_03, g_12 = jnp.where(outer, g_mine, g_other), jnp.where(outer, g_other, g_mine)
    g_all = jnp.stack([g_03[0], g_12[0], g_12[1], g_03[1]])
    return noise_target, data_target, f_both.reshape(-1), g_all.reshape(-1)


def solution(mesh):
    torus = Mesh(mesh.devices.reshape(4, 4, 4, 2), ALL)
    return jax.shard_map(
        shards,
        mesh=torus,
        in_specs=(P(("y", "z", "x", "c"), None), P(("x", "c", "y", "z"), None)),
        out_specs=(
            P(("y", "z", "x", "c"), None),
            P(("x", "c", "y", "z"), None),
            P(("y", "z")),
            P(("x", "c")),
        ),
        check_vma=False,
    )
```

profile of v0, /device:TPU:0, one launch (start us, length us, event | category | flops | bytes accessed | tf_op | source)
XLA Modules:
  0.0 182.7 jit_solution(14708548895220761189)
XLA Ops:
  0.6 2.9 %collective-permute-start.1 = (f32[128,512]{1,0:T(8,128)}, f32[128,512]{1,0:T(8,128)S(1)}, u32[]{:S(2)}, u32[]{:S(2)}) collective-permute-start(f32[128,512]{1,0:T(8,128)} %refs_1_.1), channel_id=1, source_target_pairs={{0,6},{2,0},{4,2},{6,4},{1,7},{3,1},{5,3},{7,5},{8,14},{10,8},{12,... | collective-permute-start | bytes 786440 | tf_op jit(solution)/shard_map/ppermute | solution.py:528
  3.5 1.6 collective-permute-start.2
  5.1 2.2 %collective-permute-start.9 = (f32[128,512]{1,0:T(8,128)}, f32[128,512]{1,0:T(8,128)S(1)}, u32[]{:S(2)}, u32[]{:S(2)}) collective-permute-start(f32[128,512]{1,0:T(8,128)} %refs_0_.1), channel_id=1, source_target_pairs={{32,64},{64,32},{0,96},{96,0},{33,65},{65,33},{1,97},{97,1},{34,66... | collective-permute-start | bytes 786440 | tf_op jit(solution)/shard_map/ppermute | solution.py:529
  7.3 2.1 %collective-permute-done.1.refs_3_ = f32[128,512]{1,0:T(8,128)S(1)} collective-permute-done((f32[128,512]{1,0:T(8,128)}, f32[128,512]{1,0:T(8,128)S(1)}, u32[]{:S(2)}, u32[]{:S(2)}) %collective-permute-start.1) | collective-permute-done | bytes 262176 | tf_op jit(solution)/shard_map/ppermute | solution.py:528
  9.4 4.0 %collective-permute-start.8 = (f32[128,512]{1,0:T(8,128)}, f32[128,512]{1,0:T(8,128)S(1)}, u32[]{:S(2)}, u32[]{:S(2)}) collective-permute-start(f32[128,512]{1,0:T(8,128)} %refs_0_.1), channel_id=1, source_target_pairs={{0,24},{8,0},{16,8},{24,16},{1,25},{9,1},{17,9},{25,17},{2,26},{10... | collective-permute-start | bytes 786440 | tf_op jit(solution)/shard_map/ppermute | solution.py:528
  13.5 1.2 collective-permute-start.7
  14.7 3.2 %collective-permute-start.5 = (f32[128,512]{1,0:T(8,128)S(1)}, f32[128,512]{1,0:T(8,128)}, u32[]{:S(2)}, u32[]{:S(2)}) collective-permute-start(f32[128,512]{1,0:T(8,128)S(1)} %collective-permute-done.2.refs_4_), channel_id=1, source_target_pairs={{0,6},{2,0},{4,2},{6,4},{1,7},{3,1},{5,3},{7,5},{8,14},{10,8},{12,... | collective-permute-start | bytes 786440 | tf_op jit(solution)/shard_map/ppermute | solution.py:532
  18.5 3.6 %collective-permute-done.7.refs_10_.refs_1_ = f32[128,512]{1,0:T(8,128)S(1)} collective-permute-done((f32[128,512]{1,0:T(8,128)}, f32[128,512]{1,0:T(8,128)S(1)}, u32[]{:S(2)}, u32[]{:S(2)}) %collective-permute-start.7) | collective-permute-done | bytes 262176 | tf_op jit(solution)/shard_map/ppermute | solution.py:527
  22.1 3.1 %collective-permute-done.3.refs_5_ = f32[128,512]{1,0:T(8,128)} collective-permute-done((f32[128,512]{1,0:T(8,128)S(1)}, f32[128,512]{1,0:T(8,128)}, u32[]{:S(2)}, u32[]{:S(2)}) %collective-permute-start.3) | collective-permute-done | bytes 262176 | tf_op jit(solution)/shard_map/ppermute | solution.py:530
  25.2 2.1 %collective-permute-start.12 = (f32[128,512]{1,0:T(8,128)S(1)}, f32[128,512]{1,0:T(8,128)S(1)}, u32[]{:S(2)}, u32[]{:S(2)}) collective-permute-start(f32[128,512]{1,0:T(8,128)S(1)} %collective-permute-done.9.refs_12_.refs_3_), channel_id=1, source_target_pairs={{0,24},{8,0},{16,8},{24,16},{1,25},{9,1},{17,9},{25,17},{2,26},{10... | collective-permute-start | bytes 786440 | tf_op jit(solution)/shard_map/ppermute | solution.py:532
  27.3 0.8 collective-permute-done.4.refs_6_
  28.1 0.7 copy-done.16
  28.8 3.6 %collective-permute-done.10.refs_13_.refs_4_ = f32[128,512]{1,0:T(8,128)S(1)} collective-permute-done((f32[128,512]{1,0:T(8,128)S(1)}, f32[128,512]{1,0:T(8,128)S(1)}, u32[]{:S(2)}, u32[]{:S(2)}) %collective-permute-start.10) | collective-permute-done | bytes 262176 | tf_op jit(solution)/shard_map/ppermute | solution.py:530
  32.4 3.0 %collective-permute-start.13 = (f32[128,512]{1,0:T(8,128)S(1)}, f32[128,512]{1,0:T(8,128)S(1)}, u32[]{:S(2)}, u32[]{:S(2)}) collective-permute-start(f32[128,512]{1,0:T(8,128)S(1)} %collective-permute-done.10.refs_13_.refs_4_), channel_id=1, source_target_pairs={{32,64},{64,32},{0,96},{96,0},{33,65},{65,33},{1,97},{97,1},{34,66... | collective-permute-start | bytes 786440 | tf_op jit(solution)/shard_map/ppermute | solution.py:533
  35.5 1.3 collective-permute-start.6
  37.3 2.7 %collective-permute-done.13.refs_16_.refs_7_ = f32[128,512]{1,0:T(8,128)S(1)} collective-permute-done((f32[128,512]{1,0:T(8,128)S(1)}, f32[128,512]{1,0:T(8,128)S(1)}, u32[]{:S(2)}, u32[]{:S(2)}) %collective-permute-start.13) | collective-permute-done | bytes 262176 | tf_op jit(solution)/shard_map/ppermute | solution.py:533
  40.3 4.2 %collective-permute-done.6.refs_8_ = f32[128,512]{1,0:T(8,128)} collective-permute-done((f32[128,512]{1,0:T(8,128)}, f32[128,512]{1,0:T(8,128)}, u32[]{:S(2)}, u32[]{:S(2)}) %collective-permute-start.6) | collective-permute-done | bytes 262176 | tf_op jit(solution)/shard_map/ppermute | solution.py:533
  45.4 13.7 %shard_map.57 = (f32[512,1024]{1,0:T(8,128)}, f32[1024,2048]{1,0:T(8,128)S(1)}, f32[1,1024]{1,0:T(1,128)S(1)}, f32[1,1024]{1,0:T(1,128)S(1)}, f32[1,2048]{1,0:T(1,128)S(1)}) custom-call(s32[24]{0:T(128)S(1)} %stack.117.refs_0_, f32[128,512]{1,0:T(8,128)} %refs_1_.1, f32[128,512]{1,0:T(8,128)} %copy-done.14, f32[128,512]{1,0:T(8,128)} %copy-done.13, ...), custom_call_target="tpu_custom_call" | custom-call | flops 6442450944 | bytes 16793600 | tf_op jit(solution)/shard_map/pallas_call | solution.py:70
  59.1 10.4 %all_to_all.20 = f32[8,8,128]{2,1,0:T(8,128)S(1)} all-to-all(f32[8,8,128]{2,1,0:T(8,128)S(1)} %broadcast_in_dim.29), channel_id=1, replica_groups={{0,2,4,6,32,34,36,38},{1,3,5,7,33,35,37,39},{8,10,12,14,40,42,44,46},{9..., dimensions={0} | all-to-all | bytes 65536 | tf_op jit(solution)/shard_map/all_to_all | solution.py:521
  69.5 4.7 %shard_map.58 = (bf16[8,1024,256]{2,1,0:T(8,128)(2,1)}, bf16[8,1024,256]{2,1,0:T(8,128)(2,1)}, f32[1,2048]{1,0:T(1,128)S(1)}, f32[1,2048]{1,0:T(1,128)S(1)}, f32[1,1024]{1,0:T(1,128)S(1)}) custom-call(f32[1024,2048]{1,0:T(8,128)S(1)} %get-tuple-element.53.s_ref, f32[8,1024]{1,0:T(8,128)S(1)} %bitcast.63), custom_call_target="tpu_custom_call" | custom-call | flops 8388608 | bytes 16830464 | tf_op jit(solution)/shard_map/pallas_call | solution.py:70
  74.4 1.1 collective-permute-done.22
  76.2 4.4 %all-to-all-start.1 = ((f32[8,16,128]{2,1,0:T(8,128)}), f32[8,16,128]{2,1,0:T(8,128)S(1)}, u32[]{:S(2)}, u32[]{:S(2)}) async-start(f32[8,16,128]{2,1,0:T(8,128)} %broadcast_in_dim.31), calls=%async_computation.1 | async-start | bytes 131072 | tf_op jit(solution)/shard_map/all_to_all | solution.py:521
  80.5 7.5 %all-to-all-done.1 = f32[8,16,128]{2,1,0:T(8,128)S(1)} async-done(((f32[8,16,128]{2,1,0:T(8,128)}), f32[8,16,128]{2,1,0:T(8,128)S(1)}, u32[]{:S(2)}, u32[]{:S(2)}) %all-to-all-start.1) | async-done | bytes 65568 | tf_op jit(solution)/shard_map/all_to_all | solution.py:521
  88.1 4.0 %shard_map.59 = (f32[1,1024]{1,0:T(1,128)S(1)}, f32[1,2048]{1,0:T(1,128)S(1)}, f32[1,2048]{1,0:T(1,128)S(1)}) custom-call(bf16[8,1024,256]{2,1,0:T(8,128)(2,1)} %get-tuple-element.55.high.high_from, bf16[8,1024,256]{2,1,0:T(8,128)(2,1)} %get-tuple-element.56.low.low_from, f32[1,2048]{1,0:T(1,128)S(1)} %get-tuple-element.57.top_ref, f32[8,2048]{1,0:T(8,128)S(1)} %bitcast.62), custom_call_target="tpu_custom_call" | custom-call | flops 8388608 | bytes 8482816 | tf_op jit(solution)/shard_map/pallas_call | solution.py:70
  92.8 3.3 %all-to-all-start.2 = ((f32[8,8,128]{2,1,0:T(8,128)}), f32[8,8,128]{2,1,0:T(8,128)S(1)}, u32[]{:S(2)}, u32[]{:S(2)}) async-start(f32[8,8,128]{2,1,0:T(8,128)} %broadcast_in_dim.33), calls=%async_computation.2 | async-start | bytes 65536 | tf_op jit(solution)/shard_map/all_to_all | solution.py:521
  96.3 6.0 %all-to-all-done.2 = f32[8,8,128]{2,1,0:T(8,128)S(1)} async-done(((f32[8,8,128]{2,1,0:T(8,128)}), f32[8,8,128]{2,1,0:T(8,128)S(1)}, u32[]{:S(2)}, u32[]{:S(2)}) %all-to-all-start.2) | async-done | bytes 32800 | tf_op jit(solution)/shard_map/all_to_all | solution.py:521
  102.3 3.7 %shard_map.60 = (f32[1,2048]{1,0:T(1,128)S(1)}, f32[1,1024]{1,0:T(1,128)S(1)}) custom-call(bf16[8,1024,256]{2,1,0:T(8,128)(2,1)} %get-tuple-element.55.high.high_from, bf16[8,1024,256]{2,1,0:T(8,128)(2,1)} %get-tuple-element.56.low.low_from, f32[8,1024]{1,0:T(8,128)S(1)} %bitcast.64, f32[1,2048]{1,0:T(1,128)S(1)} %get-tuple-element.60.t_ref.refs_17_), custom_call_target="tpu_custom_call" | custom-call | flops 8388608 | bytes 8441856 | tf_op jit(solution)/shard_map/pallas_call | solution.py:70
  106.1 8.0 %shard_map.62 = (f32[128,512]{1,0:T(8,128)S(1)}, f32[128,512]{1,0:T(8,128)S(1)}, f32[128,512]{1,0:T(8,128)S(1)}, f32[128,512]{1,0:T(8,128)S(1)}, f32[128,512]{1,...) custom-call(s32[17]{0:T(128)S(1)} %get-tuple-element.106.seats, ...), custom_call_target="tpu_custom_call" | custom-call | flops 3221225472 | bytes 12595200 | tf_op jit(solution)/shard_map/pallas_call | solution.py:70
  115.2 8.0 %shard_map.61 = (f32[128,512]{1,0:T(8,128)S(1)}, f32[128,512]{1,0:T(8,128)S(1)}, f32[128,512]{1,0:T(8,128)S(1)}, f32[128,512]{1,0:T(8,128)S(1)}, f32[128,512]{1,...) custom-call(s32[17]{0:T(128)S(1)} %get-tuple-element.107.seats, ...), custom_call_target="tpu_custom_call" | custom-call | flops 3221225472 | bytes 12595200 | tf_op jit(solution)/shard_map/pallas_call | solution.py:70
  127.0 3.4 %all-to-all-start.3 = ((f32[8,16,128]{2,1,0:T(8,128)}), f32[8,16,128]{2,1,0:T(8,128)S(1)}, u32[]{:S(2)}, u32[]{:S(2)}) async-start(f32[8,16,128]{2,1,0:T(8,128)} %broadcast_in_dim.35), calls=%async_computation.3 | async-start | bytes 131072 | tf_op jit(solution)/shard_map/all_to_all | solution.py:521
  131.0 1.9 %collective-permute-start.40 = (f32[128,512]{1,0:T(8,128)S(1)}, f32[128,512]{1,0:T(8,128)S(1)}, u32[]{:S(2)}, u32[]{:S(2)}) collective-permute-start(f32[128,512]{1,0:T(8,128)S(1)} %add.351), channel_id=1, source_target_pairs={{0,8},{8,16},{16,24},{24,0},{1,9},{9,17},{17,25},{25,1},{2,10},{10... | collective-permute-start | bytes 786440 | tf_op jit(solution)/shard_map/ppermute | solution.py:541
  132.9 1.3 collective-permute-start.41
  134.2 3.1 %collective-permute-start.43 = (f32[128,512]{1,0:T(8,128)S(1)}, f32[128,512]{1,0:T(8,128)S(1)}, u32[]{:S(2)}, u32[]{:S(2)}) collective-permute-start(f32[128,512]{1,0:T(8,128)S(1)} %add.352), channel_id=1, source_target_pairs={{32,64},{64,32},{0,96},{96,0},{33,65},{65,33},{1,97},{97,1},{34,66... | collective-permute-start | bytes 786440 | tf_op jit(solution)/shard_map/ppermute | solution.py:540
  138.0 15.3 %shard_map.63 = (f32[136,512]{1,0:T(8,128)S(1)}, f32[136,512]{1,0:T(8,128)S(1)}, f32[136,512]{1,0:T(8,128)S(1)}, f32[136,512]{1,0:T(8,128)S(1)}, f32[136,512]{1,...) custom-call(s32[24]{0:T(128)S(1)} %concatenate.11.seats, ...), custom_call_target="tpu_custom_call" | custom-call | flops 6442450944 | bytes 14893056 | tf_op jit(solution)/shard_map/pallas_call | solution.py:70
  153.4 2.0 %collective-permute-start.36 = (f32[136,512]{1,0:T(8,128)S(1)}, f32[136,512]{1,0:T(8,128)S(1)}, u32[]{:S(2)}, u32[]{:S(2)}) collective-permute-start(f32[136,512]{1,0:T(8,128)S(1)} %get-tuple-element.88), channel_id=1, source_target_pairs={{0,32},{32,0},{64,96},{96,64},{1,33},{33,1},{65,97},{97,65},{2,34}... | collective-permute-start | bytes 835592 | tf_op jit(solution)/shard_map/ppermute | solution.py:540
  155.5 1.7 collective-permute-done.47
  157.8 2.6 %collective-permute-start.34 = (f32[136,512]{1,0:T(8,128)S(1)}, f32[136,512]{1,0:T(8,128)S(1)}, u32[]{:S(2)}, u32[]{:S(2)}) collective-permute-start(f32[136,512]{1,0:T(8,128)S(1)} %get-tuple-element.85), channel_id=1, source_target_pairs={{0,6},{2,0},{4,2},{6,4},{1,7},{3,1},{5,3},{7,5},{8,14},{10,8},{12,... | collective-permute-start | bytes 835592 | tf_op jit(solution)/shard_map/ppermute | solution.py:541
  161.9 2.6 %collective-permute-start.39 = (f32[128,512]{1,0:T(8,128)S(1)}, f32[128,512]{1,0:T(8,128)S(1)}, u32[]{:S(2)}, u32[]{:S(2)}) collective-permute-start(f32[128,512]{1,0:T(8,128)S(1)} %add.349), channel_id=1, source_target_pairs={{0,24},{8,0},{16,8},{24,16},{1,25},{9,1},{17,9},{25,17},{2,26},{10... | collective-permute-start | bytes 786440 | tf_op jit(solution)/shard_map/ppermute | solution.py:543
  165.2 3.5 %collective-permute-done.44 = f32[128,512]{1,0:T(8,128)S(1)} collective-permute-done((f32[128,512]{1,0:T(8,128)S(1)}, f32[128,512]{1,0:T(8,128)S(1)}, u32[]{:S(2)}, u32[]{:S(2)}) %collective-permute-start.44) | collective-permute-done | bytes 262176 | tf_op jit(solution)/shard_map/ppermute | solution.py:542
  168.7 1.2 collective-permute-start.32
  170.0 0.8 collective-permute-start.42
  170.9 1.4 collective-permute-done.37
  172.3 1.7 collective-permute-start.35
  174.6 3.0 %collective-permute-done.42 = f32[128,512]{1,0:T(8,128)S(1)} collective-permute-done((f32[128,512]{1,0:T(8,128)S(1)}, f32[128,512]{1,0:T(8,128)S(1)}, u32[]{:S(2)}, u32[]{:S(2)}) %collective-permute-start.42) | collective-permute-done | bytes 262176 | tf_op jit(solution)/shard_map/ppermute | solution.py:544
  177.6 0.8 collective-permute-done.45
  178.4 0.8 add_divide_fusion
  179.2 2.6 %collective-permute-done.38 = f32[136,512]{1,0:T(8,128)S(1)} collective-permute-done((f32[136,512]{1,0:T(8,128)S(1)}, f32[136,512]{1,0:T(8,128)S(1)}, u32[]{:S(2)}, u32[]{:S(2)}) %collective-permute-start.38) | collective-permute-done | bytes 278560 | tf_op jit(solution)/shard_map/ppermute | solution.py:544
  181.9 0.8 slice_divide_fusion
  (140 shorter events, 13.6 us)
Async XLA Ops:
  0.6 8.8 %collective-permute-start.1 = (f32[128,512]{1,0:T(8,128)}, f32[128,512]{1,0:T(8,128)S(1)}, u32[]{:S(2)}, u32[]{:S(2)}) collective-permute-start(f32[128,512]{1,0:T(8,128)} %refs_1_.1), channel_id=1, source_target_pairs={{0,6},{2,0},{4,2},{6,4},{1,7},{3,1},{5,3},{7,5},{8,14},{10,8},{12,... | collective-permute-start | bytes 786440 | tf_op jit(solution)/shard_map/ppermute | solution.py:528
  3.5 9.9 %collective-permute-start = (f32[128,512]{1,0:T(8,128)}, f32[128,512]{1,0:T(8,128)S(1)}, u32[]{:S(2)}, u32[]{:S(2)}) collective-permute-start(f32[128,512]{1,0:T(8,128)} %refs_1_.1), channel_id=1, source_target_pairs={{0,2},{2,4},{4,6},{6,0},{1,3},{3,5},{5,7},{7,1},{8,10},{10,12},{12... | collective-permute-start | bytes 786440 | tf_op jit(solution)/shard_map/ppermute | solution.py:527
  3.5 11.1 %collective-permute-start.2 = (f32[128,512]{1,0:T(8,128)}, f32[128,512]{1,0:T(8,128)S(1)}, u32[]{:S(2)}, u32[]{:S(2)}) collective-permute-start(f32[128,512]{1,0:T(8,128)} %refs_1_.1), channel_id=1, source_target_pairs={{0,32},{32,0},{64,96},{96,64},{1,33},{33,1},{65,97},{97,65},{2,34}... | collective-permute-start | bytes 786440 | tf_op jit(solution)/shard_map/ppermute | solution.py:529
  5.1 9.6 %collective-permute-start.14 = (f32[128,512]{1,0:T(8,128)}, f32[128,512]{1,0:T(8,128)S(1)}, u32[]{:S(2)}, u32[]{:S(2)}) collective-permute-start(f32[128,512]{1,0:T(8,128)} %refs_0_.1), channel_id=1, source_target_pairs={{0,1},{1,0},{2,3},{3,2},{4,5},{5,4},{6,7},{7,6},{8,9},{9,8},{10,11... | collective-permute-start | bytes 786440 | tf_op jit(solution)/shard_map/ppermute | solution.py:553
  5.1 12.8 %collective-permute-start.9 = (f32[128,512]{1,0:T(8,128)}, f32[128,512]{1,0:T(8,128)S(1)}, u32[]{:S(2)}, u32[]{:S(2)}) collective-permute-start(f32[128,512]{1,0:T(8,128)} %refs_0_.1), channel_id=1, source_target_pairs={{32,64},{64,32},{0,96},{96,0},{33,65},{65,33},{1,97},{97,1},{34,66... | collective-permute-start | bytes 786440 | tf_op jit(solution)/shard_map/ppermute | solution.py:529
  9.4 9.0 %collective-permute-start.8 = (f32[128,512]{1,0:T(8,128)}, f32[128,512]{1,0:T(8,128)S(1)}, u32[]{:S(2)}, u32[]{:S(2)}) collective-permute-start(f32[128,512]{1,0:T(8,128)} %refs_0_.1), channel_id=1, source_target_pairs={{0,24},{8,0},{16,8},{24,16},{1,25},{9,1},{17,9},{25,17},{2,26},{10... | collective-permute-start | bytes 786440 | tf_op jit(solution)/shard_map/ppermute | solution.py:528
  13.5 8.6 %collective-permute-start.7 = (f32[128,512]{1,0:T(8,128)}, f32[128,512]{1,0:T(8,128)S(1)}, u32[]{:S(2)}, u32[]{:S(2)}) collective-permute-start(f32[128,512]{1,0:T(8,128)} %refs_0_.1), channel_id=1, source_target_pairs={{0,8},{8,16},{16,24},{24,0},{1,9},{9,17},{17,25},{25,1},{2,10},{10... | collective-permute-start | bytes 786440 | tf_op jit(solution)/shard_map/ppermute | solution.py:527
  14.7 10.6 %collective-permute-start.3 = (f32[128,512]{1,0:T(8,128)S(1)}, f32[128,512]{1,0:T(8,128)}, u32[]{:S(2)}, u32[]{:S(2)}) collective-permute-start(f32[128,512]{1,0:T(8,128)S(1)} %collective-permute-done.refs_2_), channel_id=1, source_target_pairs={{0,2},{2,4},{4,6},{6,0},{1,3},{3,5},{5,7},{7,1},{8,10},{10,12},{12... | collective-permute-start | bytes 786440 | tf_op jit(solution)/shard_map/ppermute | solution.py:530
  14.7 12.6 %collective-permute-start.5 = (f32[128,512]{1,0:T(8,128)S(1)}, f32[128,512]{1,0:T(8,128)}, u32[]{:S(2)}, u32[]{:S(2)}) collective-permute-start(f32[128,512]{1,0:T(8,128)S(1)} %collective-permute-done.2.refs_4_), channel_id=1, source_target_pairs={{0,6},{2,0},{4,2},{6,4},{1,7},{3,1},{5,3},{7,5},{8,14},{10,8},{12,... | collective-permute-start | bytes 786440 | tf_op jit(solution)/shard_map/ppermute | solution.py:532
  17.9 10.2 %collective-permute-start.4 = (f32[128,512]{1,0:T(8,128)S(1)}, f32[128,512]{1,0:T(8,128)S(1)}, u32[]{:S(2)}, u32[]{:S(2)}) collective-permute-start(f32[128,512]{1,0:T(8,128)S(1)} %collective-permute-done.2.refs_4_), channel_id=1, source_target_pairs={{0,2},{2,4},{4,6},{6,0},{1,3},{3,5},{5,7},{7,1},{8,10},{10,12},{12... | collective-permute-start | bytes 786440 | tf_op jit(solution)/shard_map/ppermute | solution.py:531
  18.5 10.3 %collective-permute-start.17 = (f32[128,512]{1,0:T(8,128)S(1)}, f32[128,512]{1,0:T(8,128)S(1)}, u32[]{:S(2)}, u32[]{:S(2)}) collective-permute-start(f32[128,512]{1,0:T(8,128)S(1)} %collective-permute-done.9.refs_12_.refs_3_), channel_id=1, source_target_pairs={{0,1},{1,0},{2,3},{3,2},{4,5},{5,4},{6,7},{7,6},{8,9},{9,8},{10,11... | collective-permute-start | bytes 786440 | tf_op jit(solution)/shard_map/ppermute | solution.py:553
  22.1 10.3 %collective-permute-start.10 = (f32[128,512]{1,0:T(8,128)S(1)}, f32[128,512]{1,0:T(8,128)S(1)}, u32[]{:S(2)}, u32[]{:S(2)}) collective-permute-start(f32[128,512]{1,0:T(8,128)S(1)} %collective-permute-done.7.refs_10_.refs_1_), channel_id=1, source_target_pairs={{0,8},{8,16},{16,24},{24,0},{1,9},{9,17},{17,25},{25,1},{2,10},{10... | collective-permute-start | bytes 786440 | tf_op jit(solution)/shard_map/ppermute | solution.py:530
  25.2 10.2 %collective-permute-start.12 = (f32[128,512]{1,0:T(8,128)S(1)}, f32[128,512]{1,0:T(8,128)S(1)}, u32[]{:S(2)}, u32[]{:S(2)}) collective-permute-start(f32[128,512]{1,0:T(8,128)S(1)} %collective-permute-done.9.refs_12_.refs_3_), channel_id=1, source_target_pairs={{0,24},{8,0},{16,8},{24,16},{1,25},{9,1},{17,9},{25,17},{2,26},{10... | collective-permute-start | bytes 786440 | tf_op jit(solution)/shard_map/ppermute | solution.py:532
  27.3 8.2 %collective-permute-start.11 = (f32[128,512]{1,0:T(8,128)S(1)}, f32[128,512]{1,0:T(8,128)S(1)}, u32[]{:S(2)}, u32[]{:S(2)}) collective-permute-start(f32[128,512]{1,0:T(8,128)S(1)} %collective-permute-done.9.refs_12_.refs_3_), channel_id=1, source_target_pairs={{0,8},{8,16},{16,24},{24,0},{1,9},{9,17},{17,25},{25,1},{2,10},{10... | collective-permute-start | bytes 786440 | tf_op jit(solution)/shard_map/ppermute | solution.py:531
  28.1 8.8 %collective-permute-start.16 = (f32[128,512]{1,0:T(8,128)S(1)}, f32[128,512]{1,0:T(8,128)S(1)}, u32[]{:S(2)}, u32[]{:S(2)}) collective-permute-start(f32[128,512]{1,0:T(8,128)S(1)} %collective-permute-done.8.refs_11_.refs_2_), channel_id=1, source_target_pairs={{0,1},{1,0},{2,3},{3,2},{4,5},{5,4},{6,7},{7,6},{8,9},{9,8},{10,11... | collective-permute-start | bytes 786440 | tf_op jit(solution)/shard_map/ppermute | solution.py:553
  28.8 8.0 %collective-permute-start.15 = (f32[128,512]{1,0:T(8,128)S(1)}, f32[128,512]{1,0:T(8,128)S(1)}, u32[]{:S(2)}, u32[]{:S(2)}) collective-permute-start(f32[128,512]{1,0:T(8,128)S(1)} %collective-permute-done.7.refs_10_.refs_1_), channel_id=1, source_target_pairs={{0,1},{1,0},{2,3},{3,2},{4,5},{5,4},{6,7},{7,6},{8,9},{9,8},{10,11... | collective-permute-start | bytes 786440 | tf_op jit(solution)/shard_map/ppermute | solution.py:553
  32.4 7.6 %collective-permute-start.13 = (f32[128,512]{1,0:T(8,128)S(1)}, f32[128,512]{1,0:T(8,128)S(1)}, u32[]{:S(2)}, u32[]{:S(2)}) collective-permute-start(f32[128,512]{1,0:T(8,128)S(1)} %collective-permute-done.10.refs_13_.refs_4_), channel_id=1, source_target_pairs={{32,64},{64,32},{0,96},{96,0},{33,65},{65,33},{1,97},{97,1},{34,66... | collective-permute-start | bytes 786440 | tf_op jit(solution)/shard_map/ppermute | solution.py:533
  35.5 9.1 %collective-permute-start.18 = (f32[128,512]{1,0:T(8,128)S(1)}, f32[128,512]{1,0:T(8,128)S(1)}, u32[]{:S(2)}, u32[]{:S(2)}) collective-permute-start(f32[128,512]{1,0:T(8,128)S(1)} %collective-permute-done.10.refs_13_.refs_4_), channel_id=1, source_target_pairs={{0,1},{1,0},{2,3},{3,2},{4,5},{5,4},{6,7},{7,6},{8,9},{9,8},{10,11... | collective-permute-start | bytes 786440 | tf_op jit(solution)/shard_map/ppermute | solution.py:553
  35.5 9.0 %collective-permute-start.6 = (f32[128,512]{1,0:T(8,128)}, f32[128,512]{1,0:T(8,128)}, u32[]{:S(2)}, u32[]{:S(2)}) collective-permute-start(f32[128,512]{1,0:T(8,128)} %collective-permute-done.3.refs_5_), channel_id=1, source_target_pairs={{0,32},{32,0},{64,96},{96,64},{1,33},{33,1},{65,97},{97,65},{2,34}... | collective-permute-start | bytes 786440 | tf_op jit(solution)/shard_map/ppermute | solution.py:533
  36.8 7.7 %collective-permute-start.20 = (f32[128,512]{1,0:T(8,128)S(1)}, f32[128,512]{1,0:T(8,128)S(1)}, u32[]{:S(2)}, u32[]{:S(2)}) collective-permute-start(f32[128,512]{1,0:T(8,128)S(1)} %collective-permute-done.12.refs_15_.refs_6_), channel_id=1, source_target_pairs={{0,1},{1,0},{2,3},{3,2},{4,5},{5,4},{6,7},{7,6},{8,9},{9,8},{10,11... | collective-permute-start | bytes 786440 | tf_op jit(solution)/shard_map/ppermute | solution.py:553
  36.9 7.7 %collective-permute-start.19 = (f32[128,512]{1,0:T(8,128)S(1)}, f32[128,512]{1,0:T(8,128)}, u32[]{:S(2)}, u32[]{:S(2)}) collective-permute-start(f32[128,512]{1,0:T(8,128)S(1)} %collective-permute-done.11.refs_14_.refs_5_), channel_id=1, source_target_pairs={{0,1},{1,0},{2,3},{3,2},{4,5},{5,4},{6,7},{7,6},{8,9},{9,8},{10,11... | collective-permute-start | bytes 786440 | tf_op jit(solution)/shard_map/ppermute | solution.py:553
  40.0 4.5 %collective-permute-start.21 = (f32[128,512]{1,0:T(8,128)S(1)}, f32[128,512]{1,0:T(8,128)}, u32[]{:S(2)}, u32[]{:S(2)}) collective-permute-start(f32[128,512]{1,0:T(8,128)S(1)} %collective-permute-done.13.refs_16_.refs_7_), channel_id=1, source_target_pairs={{0,1},{1,0},{2,3},{3,2},{4,5},{5,4},{6,7},{7,6},{8,9},{9,8},{10,11... | collective-permute-start | bytes 786440 | tf_op jit(solution)/shard_map/ppermute | solution.py:553
  76.2 11.9 %all-to-all-start.1 = ((f32[8,16,128]{2,1,0:T(8,128)}), f32[8,16,128]{2,1,0:T(8,128)S(1)}, u32[]{:S(2)}, u32[]{:S(2)}) async-start(f32[8,16,128]{2,1,0:T(8,128)} %broadcast_in_dim.31), calls=%async_computation.1 | async-start | bytes 131072 | tf_op jit(solution)/shard_map/all_to_all | solution.py:521
  92.8 9.5 %all-to-all-start.2 = ((f32[8,8,128]{2,1,0:T(8,128)}), f32[8,8,128]{2,1,0:T(8,128)S(1)}, u32[]{:S(2)}, u32[]{:S(2)}) async-start(f32[8,8,128]{2,1,0:T(8,128)} %broadcast_in_dim.33), calls=%async_computation.2 | async-start | bytes 65536 | tf_op jit(solution)/shard_map/all_to_all | solution.py:521
  106.0 17.3 %collective-permute-start.23 = (f32[1,2048]{1,0:T(1,128)S(1)}, f32[1,2048]{1,0:T(1,128)S(1)}, u32[]{:S(2)}, u32[]{:S(2)}) collective-permute-start(f32[1,2048]{1,0:T(1,128)S(1)} %get-tuple-element.61), channel_id=1, source_target_pairs={{0,1},{1,0},{2,3},{3,2},{4,5},{5,4},{6,7},{7,6},{8,9},{9,8},{10,11... | collective-permute-start | bytes 24584 | tf_op jit(solution)/shard_map/ppermute | solution.py:572
  114.1 9.7 %collective-permute-start.24 = (f32[128,512]{1,0:T(8,128)S(1)}, f32[128,512]{1,0:T(8,128)S(1)}, u32[]{:S(2)}, u32[]{:S(2)}) collective-permute-start(f32[128,512]{1,0:T(8,128)S(1)} %get-tuple-element.65), channel_id=1, source_target_pairs={{0,1},{1,0},{2,3},{3,2},{4,5},{5,4},{6,7},{7,6},{8,9},{9,8},{10,11... | collective-permute-start | bytes 786440 | tf_op jit(solution)/shard_map/ppermute | solution.py:575
  114.7 9.2 %collective-permute-start.25 = (f32[128,512]{1,0:T(8,128)S(1)}, f32[128,512]{1,0:T(8,128)S(1)}, u32[]{:S(2)}, u32[]{:S(2)}) collective-permute-start(f32[128,512]{1,0:T(8,128)S(1)} %get-tuple-element.67), channel_id=1, source_target_pairs={{0,1},{1,0},{2,3},{3,2},{4,5},{5,4},{6,7},{7,6},{8,9},{9,8},{10,11... | collective-permute-start | bytes 786440 | tf_op jit(solution)/shard_map/ppermute | solution.py:575
  114.8 9.5 %collective-permute-start.26 = (f32[128,512]{1,0:T(8,128)S(1)}, f32[128,512]{1,0:T(8,128)S(1)}, u32[]{:S(2)}, u32[]{:S(2)}) collective-permute-start(f32[128,512]{1,0:T(8,128)S(1)} %get-tuple-element.69), channel_id=1, source_target_pairs={{0,1},{1,0},{2,3},{3,2},{4,5},{5,4},{6,7},{7,6},{8,9},{9,8},{10,11... | collective-permute-start | bytes 786440 | tf_op jit(solution)/shard_map/ppermute | solution.py:575
  123.4 1.8 collective-permute-start.28
  123.9 2.0 %collective-permute-start.30 = (f32[128,512]{1,0:T(8,128)S(1)}, f32[128,512]{1,0:T(8,128)S(1)}, u32[]{:S(2)}, u32[]{:S(2)}) collective-permute-start(f32[128,512]{1,0:T(8,128)S(1)} %get-tuple-element.77), channel_id=1, source_target_pairs={{0,1},{1,0},{2,3},{3,2},{4,5},{5,4},{6,7},{7,6},{8,9},{9,8},{10,11... | collective-permute-start | bytes 786440 | tf_op jit(solution)/shard_map/ppermute | solution.py:575
  124.3 2.0 %collective-permute-start.31 = (f32[128,512]{1,0:T(8,128)S(1)}, f32[128,512]{1,0:T(8,128)S(1)}, u32[]{:S(2)}, u32[]{:S(2)}) collective-permute-start(f32[128,512]{1,0:T(8,128)S(1)} %get-tuple-element.79), channel_id=1, source_target_pairs={{0,1},{1,0},{2,3},{3,2},{4,5},{5,4},{6,7},{7,6},{8,9},{9,8},{10,11... | collective-permute-start | bytes 786440 | tf_op jit(solution)/shard_map/ppermute | solution.py:575
  124.8 5.5 %collective-permute-start.46 = (f32[4,128]{1,0:T(4,128)S(1)}, f32[4,128]{1,0:T(4,128)S(1)}, u32[]{:S(2)}, u32[]{:S(2)}) collective-permute-start(f32[4,128]{1,0:T(4,128)S(1)} %fusion.9), channel_id=1, source_target_pairs={{0,1},{1,0},{2,3},{3,2},{4,5},{5,4},{6,7},{7,6},{8,9},{9,8},{10,11... | collective-permute-start | bytes 6152 | tf_op jit(solution)/shard_map/ppermute | solution.py:589
  127.0 11.0 %all-to-all-start.3 = ((f32[8,16,128]{2,1,0:T(8,128)}), f32[8,16,128]{2,1,0:T(8,128)S(1)}, u32[]{:S(2)}, u32[]{:S(2)}) async-start(f32[8,16,128]{2,1,0:T(8,128)} %broadcast_in_dim.35), calls=%async_computation.3 | async-start | bytes 131072 | tf_op jit(solution)/shard_map/all_to_all | solution.py:521
  131.0 30.9 %collective-permute-start.40 = (f32[128,512]{1,0:T(8,128)S(1)}, f32[128,512]{1,0:T(8,128)S(1)}, u32[]{:S(2)}, u32[]{:S(2)}) collective-permute-start(f32[128,512]{1,0:T(8,128)S(1)} %add.351), channel_id=1, source_target_pairs={{0,8},{8,16},{16,24},{24,0},{1,9},{9,17},{17,25},{25,1},{2,10},{10... | collective-permute-start | bytes 786440 | tf_op jit(solution)/shard_map/ppermute | solution.py:541
  132.9 31.6 %collective-permute-start.41 = (f32[128,512]{1,0:T(8,128)S(1)}, f32[128,512]{1,0:T(8,128)S(1)}, u32[]{:S(2)}, u32[]{:S(2)}) collective-permute-start(f32[128,512]{1,0:T(8,128)S(1)} %add.353), channel_id=1, source_target_pairs={{0,24},{8,0},{16,8},{24,16},{1,25},{9,1},{17,9},{25,17},{2,26},{10... | collective-permute-start | bytes 786440 | tf_op jit(solution)/shard_map/ppermute | solution.py:541
  134.2 23.6 %collective-permute-start.43 = (f32[128,512]{1,0:T(8,128)S(1)}, f32[128,512]{1,0:T(8,128)S(1)}, u32[]{:S(2)}, u32[]{:S(2)}) collective-permute-start(f32[128,512]{1,0:T(8,128)S(1)} %add.352), channel_id=1, source_target_pairs={{32,64},{64,32},{0,96},{96,0},{33,65},{65,33},{1,97},{97,1},{34,66... | collective-permute-start | bytes 786440 | tf_op jit(solution)/shard_map/ppermute | solution.py:540
  153.4 3.8 %collective-permute-start.47 = (f32[2,4,128]{2,1,0:T(4,128)S(1)}, f32[2,4,128]{2,1,0:T(4,128)S(1)}, u32[]{:S(2)}, u32[]{:S(2)}) collective-permute-start(f32[2,4,128]{2,1,0:T(4,128)S(1)} %dynamic-slice_bitcast_fusion), channel_id=1, source_target_pairs={{0,32},{32,0},{64,96},{96,64},{1,33},{33,1},{65,97},{97,65},{2,34}... | collective-permute-start | bytes 12296 | tf_op jit(solution)/shard_map/ppermute | solution.py:593
  153.4 7.7 %collective-permute-start.36 = (f32[136,512]{1,0:T(8,128)S(1)}, f32[136,512]{1,0:T(8,128)S(1)}, u32[]{:S(2)}, u32[]{:S(2)}) collective-permute-start(f32[136,512]{1,0:T(8,128)S(1)} %get-tuple-element.88), channel_id=1, source_target_pairs={{0,32},{32,0},{64,96},{96,64},{1,33},{33,1},{65,97},{97,65},{2,34}... | collective-permute-start | bytes 835592 | tf_op jit(solution)/shard_map/ppermute | solution.py:540
  157.1 12.8 %collective-permute-start.33 = (f32[136,512]{1,0:T(8,128)S(1)}, f32[136,512]{1,0:T(8,128)S(1)}, u32[]{:S(2)}, u32[]{:S(2)}) collective-permute-start(f32[136,512]{1,0:T(8,128)S(1)} %get-tuple-element.84), channel_id=1, source_target_pairs={{0,2},{2,4},{4,6},{6,0},{1,3},{3,5},{5,7},{7,1},{8,10},{10,12},{12... | collective-permute-start | bytes 835592 | tf_op jit(solution)/shard_map/ppermute | solution.py:541
  157.8 13.0 %collective-permute-start.34 = (f32[136,512]{1,0:T(8,128)S(1)}, f32[136,512]{1,0:T(8,128)S(1)}, u32[]{:S(2)}, u32[]{:S(2)}) collective-permute-start(f32[136,512]{1,0:T(8,128)S(1)} %get-tuple-element.85), channel_id=1, source_target_pairs={{0,6},{2,0},{4,2},{6,4},{1,7},{3,1},{5,3},{7,5},{8,14},{10,8},{12,... | collective-permute-start | bytes 835592 | tf_op jit(solution)/shard_map/ppermute | solution.py:541
  161.1 7.6 %collective-permute-start.44 = (f32[128,512]{1,0:T(8,128)S(1)}, f32[128,512]{1,0:T(8,128)S(1)}, u32[]{:S(2)}, u32[]{:S(2)}) collective-permute-start(f32[128,512]{1,0:T(8,128)S(1)} %add.365), channel_id=1, source_target_pairs={{0,8},{8,16},{16,24},{24,0},{1,9},{9,17},{17,25},{25,1},{2,10},{10... | collective-permute-start | bytes 786440 | tf_op jit(solution)/shard_map/ppermute | solution.py:542
  161.9 12.1 %collective-permute-start.39 = (f32[128,512]{1,0:T(8,128)S(1)}, f32[128,512]{1,0:T(8,128)S(1)}, u32[]{:S(2)}, u32[]{:S(2)}) collective-permute-start(f32[128,512]{1,0:T(8,128)S(1)} %add.349), channel_id=1, source_target_pairs={{0,24},{8,0},{16,8},{24,16},{1,25},{9,1},{17,9},{25,17},{2,26},{10... | collective-permute-start | bytes 786440 | tf_op jit(solution)/shard_map/ppermute | solution.py:543
  164.5 7.8 %collective-permute-start.37 = (f32[136,512]{1,0:T(8,128)S(1)}, f32[136,512]{1,0:T(8,128)S(1)}, u32[]{:S(2)}, u32[]{:S(2)}) collective-permute-start(f32[136,512]{1,0:T(8,128)S(1)} %add.358), channel_id=1, source_target_pairs={{0,2},{2,4},{4,6},{6,0},{1,3},{3,5},{5,7},{7,1},{8,10},{10,12},{12... | collective-permute-start | bytes 835592 | tf_op jit(solution)/shard_map/ppermute | solution.py:542
  168.7 10.5 %collective-permute-start.32 = (f32[136,512]{1,0:T(8,128)S(1)}, f32[136,512]{1,0:T(8,128)S(1)}, u32[]{:S(2)}, u32[]{:S(2)}) collective-permute-start(f32[136,512]{1,0:T(8,128)S(1)} %get-tuple-element.82), channel_id=1, source_target_pairs={{0,6},{2,0},{4,2},{6,4},{1,7},{3,1},{5,3},{7,5},{8,14},{10,8},{12,... | collective-permute-start | bytes 835592 | tf_op jit(solution)/shard_map/ppermute | solution.py:543
  170.0 7.7 %collective-permute-start.42 = (f32[128,512]{1,0:T(8,128)S(1)}, f32[128,512]{1,0:T(8,128)S(1)}, u32[]{:S(2)}, u32[]{:S(2)}) collective-permute-start(f32[128,512]{1,0:T(8,128)S(1)} %add_add_fusion.2), channel_id=1, source_target_pairs={{32,64},{64,32},{0,96},{96,0},{33,65},{65,33},{1,97},{97,1},{34,66... | collective-permute-start | bytes 786440 | tf_op jit(solution)/shard_map/ppermute | solution.py:544
  170.8 7.6 %collective-permute-start.45 = (f32[128,512]{1,0:T(8,128)S(1)}, f32[128,512]{1,0:T(8,128)S(1)}, u32[]{:S(2)}, u32[]{:S(2)}) collective-permute-start(f32[128,512]{1,0:T(8,128)S(1)} %add.366), channel_id=1, source_target_pairs={{0,8},{8,16},{16,24},{24,0},{1,9},{9,17},{17,25},{25,1},{2,10},{10... | collective-permute-start | bytes 786440 | tf_op jit(solution)/shard_map/ppermute | solution.py:544
  172.3 7.0 %collective-permute-start.35 = (f32[136,512]{1,0:T(8,128)S(1)}, f32[136,512]{1,0:T(8,128)S(1)}, u32[]{:S(2)}, u32[]{:S(2)}) collective-permute-start(f32[136,512]{1,0:T(8,128)S(1)} %add_add_fusion.1), channel_id=1, source_target_pairs={{0,32},{32,0},{64,96},{96,64},{1,33},{33,1},{65,97},{97,65},{2,34}... | collective-permute-start | bytes 835592 | tf_op jit(solution)/shard_map/ppermute | solution.py:544
  174.0 7.8 %collective-permute-start.38 = (f32[136,512]{1,0:T(8,128)S(1)}, f32[136,512]{1,0:T(8,128)S(1)}, u32[]{:S(2)}, u32[]{:S(2)}) collective-permute-start(f32[136,512]{1,0:T(8,128)S(1)} %add.359), channel_id=1, source_target_pairs={{0,2},{2,4},{4,6},{6,0},{1,3},{3,5},{5,7},{7,1},{8,10},{10,12},{12... | collective-permute-start | bytes 835592 | tf_op jit(solution)/shard_map/ppermute | solution.py:544
  (20 other events, 230.5 us)
where the time goes:
time: 183 us
  Pallas kernels  57.5 us (31%)
  starting transfers between devices  55.2 us (30%)
  waiting for transfers between devices  51 us (28%)
  blocking collectives  10.4 us (6%)
  other arithmetic  3.68 us (2%)
  local copies, waits for them, and re-layouts  3.65 us (2%)
    pallas_call x7, Pallas kernels, call(): pl.pallas_call(kernel, in_specs=[smem] * len(scalars) + [anywhere] * len(...  57.5 us
    all_to_all x3, waiting for transfers between devices, gathered(): lax.all_to_all(mine, ALL, 0, 0, axis_index_groups=groups, tiled=True)  14.1 us
    all_to_all x3, starting transfers between devices, gathered(): lax.all_to_all(mine, ALL, 0, 0, axis_index_groups=groups, tiled=True)  11.1 us
    all_to_all x1, blocking collectives, gathered(): lax.all_to_all(mine, ALL, 0, 0, axis_index_groups=groups, tiled=True)  10.4 us
    ppermute x2, starting transfers between devices, spread(): above = lax.ppermute(own, ring, DOWN)  6.95 us
    ppermute x2, waiting for transfers between devices, spread(): over_far = lax.ppermute(far, 'y', across)  6.91 us
    ppermute x2, waiting for transfers between devices, spread(): far = lax.ppermute(below, ring, UP)  6.73 us
    ppermute x2, starting transfers between devices, spread(): over_above = lax.ppermute(over, ring, DOWN)  5.29 us
  transfers between devices with their start and end apart: 51, of which 23 were waited for; matrix products, arithmetic and copies ran while one was open for 2% of the time, Pallas kernels for 17%

commit v1 on v0

--- a/solution.py
+++ b/solution.py
@@ -39,8 +39,16 @@
 SCALE = LOG2E / EPSILON
 BLOCK = 256
 WIDE = 512
+TALL = 512
 CHUNK = 64
 VMEM_LIMIT = 32 * 1024 * 1024
+
+
+SAME_COLUMNS_BOTH = [
+    [place(y, z, x, c) for c in range(2) for y in pair for z in range(4)]
+    for pair in PAIRS_B
+    for x in range(4)
+]
 
 
 def split(v):
@@ -105,6 +113,12 @@
         copy.wait()
 
 
+def store_for_all(ref, line):
+    for k in range(ref.shape[1]):
+        values = line[:, k * 128 : (k + 1) * 128]
+        ref[:, k : k + 1, :] = jnp.broadcast_to(values.reshape(1, 1, 128), (ref.shape[0], 1, 128))
+
+
 def span(k, size):
     return pl.ds(pl.multiple_of(k * size, size), size)
 
@@ -193,7 +207,7 @@
     collect(steps - 1)
     top = jnp.max(peak[...], axis=1, keepdims=True)
     sums = jnp.sum(total[...] * jnp.exp2(peak[...] - top), axis=1, keepdims=True)
-    lse_ref[...] = as_row(jnp.broadcast_to(top + jnp.log2(sums), peak.shape))
+    store_for_all(lse_ref, as_row(jnp.broadcast_to(top + jnp.log2(sums), peak.shape)))
     kept.wait()
 
 
@@ -202,7 +216,7 @@
     return call(
         scores_kernel,
         (),
-        (f32(w, n), f32(n, m), f32(1, n), f32(1, n), f32(1, m)),
+        (f32(w, n), f32(n, m), f32(8, n // 128, 128), f32(1, n), f32(1, m)),
         (
             pltpu.VMEM((n, 3 * w), jnp.bfloat16),
             pltpu.VMEM((m, 3 * w), jnp.bfloat16),
@@ -254,7 +268,11 @@
             total = total + folded(q, jnp.sum)
             qh_ref[j, i : i + CHUNK, :], ql_ref[j, i : i + CHUNK, :] = split(q)
         top_ref[:, at] = top
-        lse_ref[:, at] = top + jnp.log2(jnp.sum(total, axis=0, keepdims=True))
+        lse = top + jnp.log2(jnp.sum(total, axis=0, keepdims=True))
+        for k in range(BLOCK // 128):
+            values = lse[:, k * 128 : (k + 1) * 128].reshape(1, 1, 128)
+            seat = pl.ds(j * (BLOCK // 128) + k, 1)
+            lse_ref[:, seat, :] = jnp.broadcast_to(values, (lse_ref.shape[0], 1, 128))
         started(kept(j))
         return carry
 
@@ -275,7 +293,7 @@
     return call(
         columns_kernel,
         (s, parts),
-        (half, half, f32(1, m), f32(1, m), f32(1, n)),
+        (half, half, f32(1, m), f32(16, m // 128, 128), f32(1, n)),
         (
             pltpu.VMEM((n, 128), jnp.float32),
             *matrix_scratch(n, m),
@@ -319,7 +337,7 @@
         return carry
 
     lax.fori_loop(0, steps, step, 0)
-    sum_ref[...] = lane_sums(total)
+    store_for_all(sum_ref, lane_sums(total))
 
 
 def row_sums(qh, ql, top, parts):
@@ -327,7 +345,7 @@
     return call(
         rows_kernel,
         (top, parts),
-        (f32(1, n), f32(1, m), f32(1, m)),
+        (f32(8, n // 128, 128), f32(1, m), f32(1, m)),
         (pltpu.VMEM((n, 128), jnp.float32), *matrix_scratch(n, m)),
         flops=4 * n * m,
         far=(qh, ql),
@@ -459,10 +477,10 @@
         return carry
 
     lax.fori_loop(0, steps, scaled, 0)
-    parts = acc.shape[0] // BLOCK
+    parts = acc.shape[0] // TALL
 
     def step(i, carry):
-        half, rows = i // parts, span(i % parts, BLOCK)
+        half, rows = i // parts, span(i % parts, TALL)
         blocks = [half * (steps // 2) + k for k in range(steps // 2)]
 
         @pl.when(i % parts == 0)
@@ -515,11 +533,14 @@
     return [p for a, b in groups for p in ((a, b), (b, a))]
 
 
+def exchanged(mine, groups):
+    parts = lax.all_to_all(mine, ALL, 0, 0, axis_index_groups=groups, tiled=True)
+    return parts.reshape(parts.shape[0], -1)
+
+
 def gathered(line, groups):
     n, size = line.shape[1], len(groups[0])
-    mine = jnp.broadcast_to(line.reshape(1, n // 128, 128), (size, n // 128, 128))
-    parts = lax.all_to_all(mine, ALL, 0, 0, axis_index_groups=groups, tiled=True)
-    return parts.reshape(size, n)
+    return exchanged(jnp.broadcast_to(line.reshape(1, n // 128, 128), (size, n // 128, 128)), groups)
 
 
 def spread(own, ring, pair):
@@ -563,12 +584,9 @@
     col_seats = ((kk // 4 % 2) ^ col_y) * 4 + (kk - iz) % 4
 
     xt, s, row_lse, xn, yn = scores_of(slots, xs, ys)
-    qh, ql, top, col_lse, a = columns_of(s, gathered(row_lse, SAME_ROWS))
-    other = lax.ppermute(col_lse, "c", CORES)
-    peak = jnp.maximum(col_lse, other)
-    col_lse = peak + jnp.log2(1.0 + jnp.exp2(jnp.minimum(col_lse, other) - peak))
-    row_part, t, b = row_sums(qh, ql, top, gathered(col_lse, SAME_COLUMNS))
-    col_part, r = column_sums(qh, ql, gathered(row_part, SAME_ROWS), t)
+    qh, ql, top, col_lse, a = columns_of(s, exchanged(row_lse, SAME_ROWS))
+    row_part, t, b = row_sums(qh, ql, top, exchanged(col_lse, SAME_COLUMNS_BOTH))
+    col_part, r = column_sums(qh, ql, exchanged(row_part, SAME_ROWS), t)
     col_part = col_part + lax.ppermute(col_part, "c", CORES)
     to_other = data_part_of(1 - ic, col_seats, qh, ql, t, r, xt)
     to_own = data_part_of(ic, col_seats, qh, ql, t, r, xt)

time: 183 us -> 181 us (0.989)
  transfers between devices with their start and end apart: 51 -> 50, of which waited for: 23 -> 22; matrix products, arithmetic and copies ran while one was open for 2% -> 2% of each run, Pallas kernels for 17% -> 17%
where the time goes in v1:
time: 181 us; the launch traced here: 180 us
  Pallas kernels  57.5 us (32%)
  starting transfers between devices  55.3 us (31%)
  waiting for transfers between devices  50 us (28%)
  blocking collectives  10.4 us (6%)
  other arithmetic  3.64 us (2%)
  local copies, waits for them, and re-layouts  2.37 us (1%)
    pallas_call x7, Pallas kernels, call(): pl.pallas_call(kernel, in_specs=[smem] * len(scalars) + [anywhere] * len(...  57.5 us
    all_to_all x3, waiting for transfers between devices, exchanged(): lax.all_to_all(mine, ALL, 0, 0, axis_index_groups=groups, tiled=True)  14.3 us
    all_to_all x3, starting transfers between devices, exchanged(): lax.all_to_all(mine, ALL, 0, 0, axis_index_groups=groups, tiled=True)  11.2 us
    all_to_all x1, blocking collectives, exchanged(): lax.all_to_all(mine, ALL, 0, 0, axis_index_groups=groups, tiled=True)  10.4 us
    ppermute x2, starting transfers between devices, spread(): above = lax.ppermute(own, ring, DOWN)  6.95 us
    ppermute x2, waiting for transfers between devices, spread(): over_far = lax.ppermute(far, 'y', across)  6.91 us
    ppermute x2, waiting for transfers between devices, spread(): far = lax.ppermute(below, ring, UP)  6.75 us
    ppermute x2, starting transfers between devices, spread(): over_above = lax.ppermute(over, ring, DOWN)  5.29 us
  transfers between devices with their start and end apart: 50, of which 22 were waited for; matrix products, arithmetic and copies ran while one was open for 2% of the time, Pallas kernels for 17%

profile of v1, /device:TPU:0, one launch (start us, length us, event | category | flops | bytes accessed | tf_op | source)
XLA Modules:
  0.0 180.5 jit_solution(14615157440293826497)
XLA Ops:
  0.6 2.9 %collective-permute-start.1 = (f32[128,512]{1,0:T(8,128)}, f32[128,512]{1,0:T(8,128)S(1)}, u32[]{:S(2)}, u32[]{:S(2)}) collective-permute-start(f32[128,512]{1,0:T(8,128)} %refs_1_.1), channel_id=1, source_target_pairs={{0,6},{2,0},{4,2},{6,4},{1,7},{3,1},{5,3},{7,5},{8,14},{10,8},{12,... | collective-permute-start | bytes 786440 | tf_op jit(solution)/shard_map/ppermute | solution.py:549
  3.5 1.6 collective-permute-start.2
  5.1 2.2 %collective-permute-start.9 = (f32[128,512]{1,0:T(8,128)}, f32[128,512]{1,0:T(8,128)S(1)}, u32[]{:S(2)}, u32[]{:S(2)}) collective-permute-start(f32[128,512]{1,0:T(8,128)} %refs_0_.1), channel_id=1, source_target_pairs={{32,64},{64,32},{0,96},{96,0},{33,65},{65,33},{1,97},{97,1},{34,66... | collective-permute-start | bytes 786440 | tf_op jit(solution)/shard_map/ppermute | solution.py:550
  7.3 2.1 %collective-permute-done.1.refs_3_ = f32[128,512]{1,0:T(8,128)S(1)} collective-permute-done((f32[128,512]{1,0:T(8,128)}, f32[128,512]{1,0:T(8,128)S(1)}, u32[]{:S(2)}, u32[]{:S(2)}) %collective-permute-start.1) | collective-permute-done | bytes 262176 | tf_op jit(solution)/shard_map/ppermute | solution.py:549
  9.4 4.0 %collective-permute-start.8 = (f32[128,512]{1,0:T(8,128)}, f32[128,512]{1,0:T(8,128)S(1)}, u32[]{:S(2)}, u32[]{:S(2)}) collective-permute-start(f32[128,512]{1,0:T(8,128)} %refs_0_.1), channel_id=1, source_target_pairs={{0,24},{8,0},{16,8},{24,16},{1,25},{9,1},{17,9},{25,17},{2,26},{10... | collective-permute-start | bytes 786440 | tf_op jit(solution)/shard_map/ppermute | solution.py:549
  13.5 1.2 collective-permute-start.7
  14.7 3.2 %collective-permute-start.5 = (f32[128,512]{1,0:T(8,128)S(1)}, f32[128,512]{1,0:T(8,128)}, u32[]{:S(2)}, u32[]{:S(2)}) collective-permute-start(f32[128,512]{1,0:T(8,128)S(1)} %collective-permute-done.2.refs_4_), channel_id=1, source_target_pairs={{0,6},{2,0},{4,2},{6,4},{1,7},{3,1},{5,3},{7,5},{8,14},{10,8},{12,... | collective-permute-start | bytes 786440 | tf_op jit(solution)/shard_map/ppermute | solution.py:553
  18.5 3.6 %collective-permute-done.7.refs_10_.refs_1_ = f32[128,512]{1,0:T(8,128)S(1)} collective-permute-done((f32[128,512]{1,0:T(8,128)}, f32[128,512]{1,0:T(8,128)S(1)}, u32[]{:S(2)}, u32[]{:S(2)}) %collective-permute-start.7) | collective-permute-done | bytes 262176 | tf_op jit(solution)/shard_map/ppermute | solution.py:548
  22.1 3.1 %collective-permute-done.3.refs_5_ = f32[128,512]{1,0:T(8,128)} collective-permute-done((f32[128,512]{1,0:T(8,128)S(1)}, f32[128,512]{1,0:T(8,128)}, u32[]{:S(2)}, u32[]{:S(2)}) %collective-permute-start.3) | collective-permute-done | bytes 262176 | tf_op jit(solution)/shard_map/ppermute | solution.py:551
  25.2 2.1 %collective-permute-start.12 = (f32[128,512]{1,0:T(8,128)S(1)}, f32[128,512]{1,0:T(8,128)S(1)}, u32[]{:S(2)}, u32[]{:S(2)}) collective-permute-start(f32[128,512]{1,0:T(8,128)S(1)} %collective-permute-done.9.refs_12_.refs_3_), channel_id=1, source_target_pairs={{0,24},{8,0},{16,8},{24,16},{1,25},{9,1},{17,9},{25,17},{2,26},{10... | collective-permute-start | bytes 786440 | tf_op jit(solution)/shard_map/ppermute | solution.py:553
  27.3 0.8 collective-permute-done.4.refs_6_
  28.1 0.7 copy-done.16
  28.8 3.6 %collective-permute-done.10.refs_13_.refs_4_ = f32[128,512]{1,0:T(8,128)S(1)} collective-permute-done((f32[128,512]{1,0:T(8,128)S(1)}, f32[128,512]{1,0:T(8,128)S(1)}, u32[]{:S(2)}, u32[]{:S(2)}) %collective-permute-start.10) | collective-permute-done | bytes 262176 | tf_op jit(solution)/shard_map/ppermute | solution.py:551
  32.4 3.0 %collective-permute-start.13 = (f32[128,512]{1,0:T(8,128)S(1)}, f32[128,512]{1,0:T(8,128)S(1)}, u32[]{:S(2)}, u32[]{:S(2)}) collective-permute-start(f32[128,512]{1,0:T(8,128)S(1)} %collective-permute-done.10.refs_13_.refs_4_), channel_id=1, source_target_pairs={{32,64},{64,32},{0,96},{96,0},{33,65},{65,33},{1,97},{97,1},{34,66... | collective-permute-start | bytes 786440 | tf_op jit(solution)/shard_map/ppermute | solution.py:554
  35.5 1.3 collective-permute-start.6
  37.3 2.7 %collective-permute-done.13.refs_16_.refs_7_ = f32[128,512]{1,0:T(8,128)S(1)} collective-permute-done((f32[128,512]{1,0:T(8,128)S(1)}, f32[128,512]{1,0:T(8,128)S(1)}, u32[]{:S(2)}, u32[]{:S(2)}) %collective-permute-start.13) | collective-permute-done | bytes 262176 | tf_op jit(solution)/shard_map/ppermute | solution.py:554
  40.3 4.2 %collective-permute-done.6.refs_8_ = f32[128,512]{1,0:T(8,128)} collective-permute-done((f32[128,512]{1,0:T(8,128)}, f32[128,512]{1,0:T(8,128)}, u32[]{:S(2)}, u32[]{:S(2)}) %collective-permute-start.6) | collective-permute-done | bytes 262176 | tf_op jit(solution)/shard_map/ppermute | solution.py:554
  45.3 13.7 %shard_map.57 = (f32[512,1024]{1,0:T(8,128)}, f32[1024,2048]{1,0:T(8,128)S(1)}, f32[8,8,128]{2,1,0:T(8,128)S(1)}, f32[1,1024]{1,0:T(1,128)S(1)}, f32[1,2048]{1,0:T(1,128)S(1)}) custom-call(s32[24]{0:T(128)S(1)} %stack.117.refs_0_, f32[128,512]{1,0:T(8,128)} %refs_1_.1, f32[128,512]{1,0:T(8,128)} %copy-done.14, f32[128,512]{1,0:T(8,128)} %copy-done.13, ...), custom_call_target="tpu_custom_call" | custom-call | flops 6442450944 | bytes 16822272 | tf_op jit(solution)/shard_map/pallas_call | solution.py:78
  59.0 10.4 %all_to_all.20 = f32[8,8,128]{2,1,0:T(8,128)S(1)} all-to-all(f32[8,8,128]{2,1,0:T(8,128)S(1)} %get-tuple-element.54), channel_id=1, replica_groups={{0,2,4,6,32,34,36,38},{1,3,5,7,33,35,37,39},{8,10,12,14,40,42,44,46},{9..., dimensions={0} | all-to-all | bytes 65536 | tf_op jit(solution)/shard_map/all_to_all | solution.py:537
  69.4 5.1 %shard_map.58 = (bf16[8,1024,256]{2,1,0:T(8,128)(2,1)}, bf16[8,1024,256]{2,1,0:T(8,128)(2,1)}, f32[1,2048]{1,0:T(1,128)S(1)}, f32[16,16,128]{2,1,0:T(8,128)}, f32[1,1024]{1,0:T(1,128)S(1)}) custom-call(f32[1024,2048]{1,0:T(8,128)S(1)} %get-tuple-element.53.s_ref, f32[8,1024]{1,0:T(8,128)S(1)} %bitcast.60), custom_call_target="tpu_custom_call" | custom-call | flops 8388608 | bytes 16953344 | tf_op jit(solution)/shard_map/pallas_call | solution.py:78
  74.5 4.5 %all-to-all-start.1 = ((f32[16,16,128]{2,1,0:T(8,128)}), f32[16,16,128]{2,1,0:T(8,128)S(1)}, u32[]{:S(2)}, u32[]{:S(2)}) async-start(f32[16,16,128]{2,1,0:T(8,128)} %get-tuple-element.58), calls=%async_computation.1 | async-start | bytes 262144 | tf_op jit(solution)/shard_map/all_to_all | solution.py:537
  79.0 7.7 %all-to-all-done.1 = f32[16,16,128]{2,1,0:T(8,128)S(1)} async-done(((f32[16,16,128]{2,1,0:T(8,128)}), f32[16,16,128]{2,1,0:T(8,128)S(1)}, u32[]{:S(2)}, u32[]{:S(2)}) %all-to-all-start.1) | async-done | bytes 131104 | tf_op jit(solution)/shard_map/all_to_all | solution.py:537
  86.8 4.6 %shard_map.59 = (f32[8,8,128]{2,1,0:T(8,128)}, f32[1,2048]{1,0:T(1,128)S(1)}, f32[1,2048]{1,0:T(1,128)S(1)}) custom-call(bf16[8,1024,256]{2,1,0:T(8,128)(2,1)} %get-tuple-element.55.high.high_from, bf16[8,1024,256]{2,1,0:T(8,128)(2,1)} %get-tuple-element.56.low.low_from, f32[1,2048]{1,0:T(1,128)S(1)} %get-tuple-element.57.top_ref, f32[16,2048]{1,0:T(8,128)S(1)} %bitcast.59), custom_call_target="tpu_custom_call" | custom-call | flops 8388608 | bytes 8577024 | tf_op jit(solution)/shard_map/pallas_call | solution.py:78
  91.4 3.4 %all-to-all-start.2 = ((f32[8,8,128]{2,1,0:T(8,128)}), f32[8,8,128]{2,1,0:T(8,128)S(1)}, u32[]{:S(2)}, u32[]{:S(2)}) async-start(f32[8,8,128]{2,1,0:T(8,128)} %get-tuple-element.59), calls=%async_computation.2 | async-start | bytes 65536 | tf_op jit(solution)/shard_map/all_to_all | solution.py:537
  95.0 6.0 %all-to-all-done.2 = f32[8,8,128]{2,1,0:T(8,128)S(1)} async-done(((f32[8,8,128]{2,1,0:T(8,128)}), f32[8,8,128]{2,1,0:T(8,128)S(1)}, u32[]{:S(2)}, u32[]{:S(2)}) %all-to-all-start.2) | async-done | bytes 32800 | tf_op jit(solution)/shard_map/all_to_all | solution.py:537
  101.0 3.7 %shard_map.60 = (f32[1,2048]{1,0:T(1,128)S(1)}, f32[1,1024]{1,0:T(1,128)S(1)}) custom-call(bf16[8,1024,256]{2,1,0:T(8,128)(2,1)} %get-tuple-element.55.high.high_from, bf16[8,1024,256]{2,1,0:T(8,128)(2,1)} %get-tuple-element.56.low.low_from, f32[8,1024]{1,0:T(8,128)S(1)} %bitcast.61, f32[1,2048]{1,0:T(1,128)S(1)} %get-tuple-element.60.t_ref.refs_17_), custom_call_target="tpu_custom_call" | custom-call | flops 8388608 | bytes 8441856 | tf_op jit(solution)/shard_map/pallas_call | solution.py:78
  104.8 8.0 %shard_map.62 = (f32[128,512]{1,0:T(8,128)S(1)}, f32[128,512]{1,0:T(8,128)S(1)}, f32[128,512]{1,0:T(8,128)S(1)}, f32[128,512]{1,0:T(8,128)S(1)}, f32[128,512]{1,...) custom-call(s32[17]{0:T(128)S(1)} %get-tuple-element.106.seats, ...), custom_call_target="tpu_custom_call" | custom-call | flops 3221225472 | bytes 12595200 | tf_op jit(solution)/shard_map/pallas_call | solution.py:78
  113.9 8.0 %shard_map.61 = (f32[128,512]{1,0:T(8,128)S(1)}, f32[128,512]{1,0:T(8,128)S(1)}, f32[128,512]{1,0:T(8,128)S(1)}, f32[128,512]{1,0:T(8,128)S(1)}, f32[128,512]{1,...) custom-call(s32[17]{0:T(128)S(1)} %get-tuple-element.107.seats, ...), custom_call_target="tpu_custom_call" | custom-call | flops 3221225472 | bytes 12595200 | tf_op jit(solution)/shard_map/pallas_call | solution.py:78
  125.7 3.4 %all-to-all-start.3 = ((f32[8,16,128]{2,1,0:T(8,128)}), f32[8,16,128]{2,1,0:T(8,128)S(1)}, u32[]{:S(2)}, u32[]{:S(2)}) async-start(f32[8,16,128]{2,1,0:T(8,128)} %broadcast_in_dim.8), calls=%async_computation.3 | async-start | bytes 131072 | tf_op jit(solution)/shard_map/all_to_all | solution.py:537
  129.7 1.9 %collective-permute-start.39 = (f32[128,512]{1,0:T(8,128)S(1)}, f32[128,512]{1,0:T(8,128)S(1)}, u32[]{:S(2)}, u32[]{:S(2)}) collective-permute-start(f32[128,512]{1,0:T(8,128)S(1)} %add.339), channel_id=1, source_target_pairs={{0,8},{8,16},{16,24},{24,0},{1,9},{9,17},{17,25},{25,1},{2,10},{10... | collective-permute-start | bytes 786440 | tf_op jit(solution)/shard_map/ppermute | solution.py:562
  131.6 1.3 collective-permute-start.40
  132.9 3.1 %collective-permute-start.42 = (f32[128,512]{1,0:T(8,128)S(1)}, f32[128,512]{1,0:T(8,128)S(1)}, u32[]{:S(2)}, u32[]{:S(2)}) collective-permute-start(f32[128,512]{1,0:T(8,128)S(1)} %add.340), channel_id=1, source_target_pairs={{32,64},{64,32},{0,96},{96,0},{33,65},{65,33},{1,97},{97,1},{34,66... | collective-permute-start | bytes 786440 | tf_op jit(solution)/shard_map/ppermute | solution.py:561
  136.7 14.4 %shard_map.63 = (f32[136,512]{1,0:T(8,128)S(1)}, f32[136,512]{1,0:T(8,128)S(1)}, f32[136,512]{1,0:T(8,128)S(1)}, f32[136,512]{1,0:T(8,128)S(1)}, f32[136,512]{1,...) custom-call(s32[24]{0:T(128)S(1)} %concatenate.11.seats, ...), custom_call_target="tpu_custom_call" | custom-call | flops 6442450944 | bytes 14893056 | tf_op jit(solution)/shard_map/pallas_call | solution.py:78
  151.2 2.0 %collective-permute-start.35 = (f32[136,512]{1,0:T(8,128)S(1)}, f32[136,512]{1,0:T(8,128)S(1)}, u32[]{:S(2)}, u32[]{:S(2)}) collective-permute-start(f32[136,512]{1,0:T(8,128)S(1)} %get-tuple-element.88), channel_id=1, source_target_pairs={{0,32},{32,0},{64,96},{96,64},{1,33},{33,1},{65,97},{97,65},{2,34}... | collective-permute-start | bytes 835592 | tf_op jit(solution)/shard_map/ppermute | solution.py:561
  153.2 1.7 collective-permute-done.46
  155.6 2.6 %collective-permute-start.33 = (f32[136,512]{1,0:T(8,128)S(1)}, f32[136,512]{1,0:T(8,128)S(1)}, u32[]{:S(2)}, u32[]{:S(2)}) collective-permute-start(f32[136,512]{1,0:T(8,128)S(1)} %get-tuple-element.85), channel_id=1, source_target_pairs={{0,6},{2,0},{4,2},{6,4},{1,7},{3,1},{5,3},{7,5},{8,14},{10,8},{12,... | collective-permute-start | bytes 835592 | tf_op jit(solution)/shard_map/ppermute | solution.py:562
  158.9 0.7 collective-permute-start.43
  159.6 2.6 %collective-permute-start.38 = (f32[128,512]{1,0:T(8,128)S(1)}, f32[128,512]{1,0:T(8,128)S(1)}, u32[]{:S(2)}, u32[]{:S(2)}) collective-permute-start(f32[128,512]{1,0:T(8,128)S(1)} %add.337), channel_id=1, source_target_pairs={{0,24},{8,0},{16,8},{24,16},{1,25},{9,1},{17,9},{25,17},{2,26},{10... | collective-permute-start | bytes 786440 | tf_op jit(solution)/shard_map/ppermute | solution.py:564
  163.0 3.5 %collective-permute-done.43 = f32[128,512]{1,0:T(8,128)S(1)} collective-permute-done((f32[128,512]{1,0:T(8,128)S(1)}, f32[128,512]{1,0:T(8,128)S(1)}, u32[]{:S(2)}, u32[]{:S(2)}) %collective-permute-start.43) | collective-permute-done | bytes 262176 | tf_op jit(solution)/shard_map/ppermute | solution.py:563
  166.5 1.2 collective-permute-start.31
  167.8 0.8 collective-permute-start.41
  168.7 1.4 collective-permute-done.36
  170.0 1.7 collective-permute-start.34
  172.4 3.0 %collective-permute-done.41 = f32[128,512]{1,0:T(8,128)S(1)} collective-permute-done((f32[128,512]{1,0:T(8,128)S(1)}, f32[128,512]{1,0:T(8,128)S(1)}, u32[]{:S(2)}, u32[]{:S(2)}) %collective-permute-start.41) | collective-permute-done | bytes 262176 | tf_op jit(solution)/shard_map/ppermute | solution.py:565
  175.4 0.8 collective-permute-done.44
  176.2 0.8 add_divide_fusion
  177.0 2.6 %collective-permute-done.37 = f32[136,512]{1,0:T(8,128)S(1)} collective-permute-done((f32[136,512]{1,0:T(8,128)S(1)}, f32[136,512]{1,0:T(8,128)S(1)}, u32[]{:S(2)}, u32[]{:S(2)}) %collective-permute-start.37) | collective-permute-done | bytes 278560 | tf_op jit(solution)/shard_map/ppermute | solution.py:565
  179.7 0.8 slice_divide_fusion
  (134 shorter events, 11.5 us)
Async XLA Ops:
  0.6 8.8 %collective-permute-start.1 = (f32[128,512]{1,0:T(8,128)}, f32[128,512]{1,0:T(8,128)S(1)}, u32[]{:S(2)}, u32[]{:S(2)}) collective-permute-start(f32[128,512]{1,0:T(8,128)} %refs_1_.1), channel_id=1, source_target_pairs={{0,6},{2,0},{4,2},{6,4},{1,7},{3,1},{5,3},{7,5},{8,14},{10,8},{12,... | collective-permute-start | bytes 786440 | tf_op jit(solution)/shard_map/ppermute | solution.py:549
  3.5 9.9 %collective-permute-start = (f32[128,512]{1,0:T(8,128)}, f32[128,512]{1,0:T(8,128)S(1)}, u32[]{:S(2)}, u32[]{:S(2)}) collective-permute-start(f32[128,512]{1,0:T(8,128)} %refs_1_.1), channel_id=1, source_target_pairs={{0,2},{2,4},{4,6},{6,0},{1,3},{3,5},{5,7},{7,1},{8,10},{10,12},{12... | collective-permute-start | bytes 786440 | tf_op jit(solution)/shard_map/ppermute | solution.py:548
  3.5 11.1 %collective-permute-start.2 = (f32[128,512]{1,0:T(8,128)}, f32[128,512]{1,0:T(8,128)S(1)}, u32[]{:S(2)}, u32[]{:S(2)}) collective-permute-start(f32[128,512]{1,0:T(8,128)} %refs_1_.1), channel_id=1, source_target_pairs={{0,32},{32,0},{64,96},{96,64},{1,33},{33,1},{65,97},{97,65},{2,34}... | collective-permute-start | bytes 786440 | tf_op jit(solution)/shard_map/ppermute | solution.py:550
  5.1 9.6 %collective-permute-start.14 = (f32[128,512]{1,0:T(8,128)}, f32[128,512]{1,0:T(8,128)S(1)}, u32[]{:S(2)}, u32[]{:S(2)}) collective-permute-start(f32[128,512]{1,0:T(8,128)} %refs_0_.1), channel_id=1, source_target_pairs={{0,1},{1,0},{2,3},{3,2},{4,5},{5,4},{6,7},{7,6},{8,9},{9,8},{10,11... | collective-permute-start | bytes 786440 | tf_op jit(solution)/shard_map/ppermute | solution.py:574
  5.1 12.8 %collective-permute-start.9 = (f32[128,512]{1,0:T(8,128)}, f32[128,512]{1,0:T(8,128)S(1)}, u32[]{:S(2)}, u32[]{:S(2)}) collective-permute-start(f32[128,512]{1,0:T(8,128)} %refs_0_.1), channel_id=1, source_target_pairs={{32,64},{64,32},{0,96},{96,0},{33,65},{65,33},{1,97},{97,1},{34,66... | collective-permute-start | bytes 786440 | tf_op jit(solution)/shard_map/ppermute | solution.py:550
  9.4 9.0 %collective-permute-start.8 = (f32[128,512]{1,0:T(8,128)}, f32[128,512]{1,0:T(8,128)S(1)}, u32[]{:S(2)}, u32[]{:S(2)}) collective-permute-start(f32[128,512]{1,0:T(8,128)} %refs_0_.1), channel_id=1, source_target_pairs={{0,24},{8,0},{16,8},{24,16},{1,25},{9,1},{17,9},{25,17},{2,26},{10... | collective-permute-start | bytes 786440 | tf_op jit(solution)/shard_map/ppermute | solution.py:549
  13.5 8.6 %collective-permute-start.7 = (f32[128,512]{1,0:T(8,128)}, f32[128,512]{1,0:T(8,128)S(1)}, u32[]{:S(2)}, u32[]{:S(2)}) collective-permute-start(f32[128,512]{1,0:T(8,128)} %refs_0_.1), channel_id=1, source_target_pairs={{0,8},{8,16},{16,24},{24,0},{1,9},{9,17},{17,25},{25,1},{2,10},{10... | collective-permute-start | bytes 786440 | tf_op jit(solution)/shard_map/ppermute | solution.py:548
  14.7 10.6 %collective-permute-start.3 = (f32[128,512]{1,0:T(8,128)S(1)}, f32[128,512]{1,0:T(8,128)}, u32[]{:S(2)}, u32[]{:S(2)}) collective-permute-start(f32[128,512]{1,0:T(8,128)S(1)} %collective-permute-done.refs_2_), channel_id=1, source_target_pairs={{0,2},{2,4},{4,6},{6,0},{1,3},{3,5},{5,7},{7,1},{8,10},{10,12},{12... | collective-permute-start | bytes 786440 | tf_op jit(solution)/shard_map/ppermute | solution.py:551
  14.7 12.6 %collective-permute-start.5 = (f32[128,512]{1,0:T(8,128)S(1)}, f32[128,512]{1,0:T(8,128)}, u32[]{:S(2)}, u32[]{:S(2)}) collective-permute-start(f32[128,512]{1,0:T(8,128)S(1)} %collective-permute-done.2.refs_4_), channel_id=1, source_target_pairs={{0,6},{2,0},{4,2},{6,4},{1,7},{3,1},{5,3},{7,5},{8,14},{10,8},{12,... | collective-permute-start | bytes 786440 | tf_op jit(solution)/shard_map/ppermute | solution.py:553
  17.9 10.2 %collective-permute-start.4 = (f32[128,512]{1,0:T(8,128)S(1)}, f32[128,512]{1,0:T(8,128)S(1)}, u32[]{:S(2)}, u32[]{:S(2)}) collective-permute-start(f32[128,512]{1,0:T(8,128)S(1)} %collective-permute-done.2.refs_4_), channel_id=1, source_target_pairs={{0,2},{2,4},{4,6},{6,0},{1,3},{3,5},{5,7},{7,1},{8,10},{10,12},{12... | collective-permute-start | bytes 786440 | tf_op jit(solution)/shard_map/ppermute | solution.py:552
  18.5 10.3 %collective-permute-start.17 = (f32[128,512]{1,0:T(8,128)S(1)}, f32[128,512]{1,0:T(8,128)S(1)}, u32[]{:S(2)}, u32[]{:S(2)}) collective-permute-start(f32[128,512]{1,0:T(8,128)S(1)} %collective-permute-done.9.refs_12_.refs_3_), channel_id=1, source_target_pairs={{0,1},{1,0},{2,3},{3,2},{4,5},{5,4},{6,7},{7,6},{8,9},{9,8},{10,11... | collective-permute-start | bytes 786440 | tf_op jit(solution)/shard_map/ppermute | solution.py:574
  22.1 10.3 %collective-permute-start.10 = (f32[128,512]{1,0:T(8,128)S(1)}, f32[128,512]{1,0:T(8,128)S(1)}, u32[]{:S(2)}, u32[]{:S(2)}) collective-permute-start(f32[128,512]{1,0:T(8,128)S(1)} %collective-permute-done.7.refs_10_.refs_1_), channel_id=1, source_target_pairs={{0,8},{8,16},{16,24},{24,0},{1,9},{9,17},{17,25},{25,1},{2,10},{10... | collective-permute-start | bytes 786440 | tf_op jit(solution)/shard_map/ppermute | solution.py:551
  25.2 10.2 %collective-permute-start.12 = (f32[128,512]{1,0:T(8,128)S(1)}, f32[128,512]{1,0:T(8,128)S(1)}, u32[]{:S(2)}, u32[]{:S(2)}) collective-permute-start(f32[128,512]{1,0:T(8,128)S(1)} %collective-permute-done.9.refs_12_.refs_3_), channel_id=1, source_target_pairs={{0,24},{8,0},{16,8},{24,16},{1,25},{9,1},{17,9},{25,17},{2,26},{10... | collective-permute-start | bytes 786440 | tf_op jit(solution)/shard_map/ppermute | solution.py:553
  27.3 8.2 %collective-permute-start.11 = (f32[128,512]{1,0:T(8,128)S(1)}, f32[128,512]{1,0:T(8,128)S(1)}, u32[]{:S(2)}, u32[]{:S(2)}) collective-permute-start(f32[128,512]{1,0:T(8,128)S(1)} %collective-permute-done.9.refs_12_.refs_3_), channel_id=1, source_target_pairs={{0,8},{8,16},{16,24},{24,0},{1,9},{9,17},{17,25},{25,1},{2,10},{10... | collective-permute-start | bytes 786440 | tf_op jit(solution)/shard_map/ppermute | solution.py:552
  28.1 8.8 %collective-permute-start.16 = (f32[128,512]{1,0:T(8,128)S(1)}, f32[128,512]{1,0:T(8,128)S(1)}, u32[]{:S(2)}, u32[]{:S(2)}) collective-permute-start(f32[128,512]{1,0:T(8,128)S(1)} %collective-permute-done.8.refs_11_.refs_2_), channel_id=1, source_target_pairs={{0,1},{1,0},{2,3},{3,2},{4,5},{5,4},{6,7},{7,6},{8,9},{9,8},{10,11... | collective-permute-start | bytes 786440 | tf_op jit(solution)/shard_map/ppermute | solution.py:574
  28.8 8.0 %collective-permute-start.15 = (f32[128,512]{1,0:T(8,128)S(1)}, f32[128,512]{1,0:T(8,128)S(1)}, u32[]{:S(2)}, u32[]{:S(2)}) collective-permute-start(f32[128,512]{1,0:T(8,128)S(1)} %collective-permute-done.7.refs_10_.refs_1_), channel_id=1, source_target_pairs={{0,1},{1,0},{2,3},{3,2},{4,5},{5,4},{6,7},{7,6},{8,9},{9,8},{10,11... | collective-permute-start | bytes 786440 | tf_op jit(solution)/shard_map/ppermute | solution.py:574
  32.4 7.6 %collective-permute-start.13 = (f32[128,512]{1,0:T(8,128)S(1)}, f32[128,512]{1,0:T(8,128)S(1)}, u32[]{:S(2)}, u32[]{:S(2)}) collective-permute-start(f32[128,512]{1,0:T(8,128)S(1)} %collective-permute-done.10.refs_13_.refs_4_), channel_id=1, source_target_pairs={{32,64},{64,32},{0,96},{96,0},{33,65},{65,33},{1,97},{97,1},{34,66... | collective-permute-start | bytes 786440 | tf_op jit(solution)/shard_map/ppermute | solution.py:554
  35.5 9.1 %collective-permute-start.18 = (f32[128,512]{1,0:T(8,128)S(1)}, f32[128,512]{1,0:T(8,128)S(1)}, u32[]{:S(2)}, u32[]{:S(2)}) collective-permute-start(f32[128,512]{1,0:T(8,128)S(1)} %collective-permute-done.10.refs_13_.refs_4_), channel_id=1, source_target_pairs={{0,1},{1,0},{2,3},{3,2},{4,5},{5,4},{6,7},{7,6},{8,9},{9,8},{10,11... | collective-permute-start | bytes 786440 | tf_op jit(solution)/shard_map/ppermute | solution.py:574
  35.5 9.0 %collective-permute-start.6 = (f32[128,512]{1,0:T(8,128)}, f32[128,512]{1,0:T(8,128)}, u32[]{:S(2)}, u32[]{:S(2)}) collective-permute-start(f32[128,512]{1,0:T(8,128)} %collective-permute-done.3.refs_5_), channel_id=1, source_target_pairs={{0,32},{32,0},{64,96},{96,64},{1,33},{33,1},{65,97},{97,65},{2,34}... | collective-permute-start | bytes 786440 | tf_op jit(solution)/shard_map/ppermute | solution.py:554
  36.8 7.7 %collective-permute-start.20 = (f32[128,512]{1,0:T(8,128)S(1)}, f32[128,512]{1,0:T(8,128)S(1)}, u32[]{:S(2)}, u32[]{:S(2)}) collective-permute-start(f32[128,512]{1,0:T(8,128)S(1)} %collective-permute-done.12.refs_15_.refs_6_), channel_id=1, source_target_pairs={{0,1},{1,0},{2,3},{3,2},{4,5},{5,4},{6,7},{7,6},{8,9},{9,8},{10,11... | collective-permute-start | bytes 786440 | tf_op jit(solution)/shard_map/ppermute | solution.py:574
  36.9 7.7 %collective-permute-start.19 = (f32[128,512]{1,0:T(8,128)S(1)}, f32[128,512]{1,0:T(8,128)}, u32[]{:S(2)}, u32[]{:S(2)}) collective-permute-start(f32[128,512]{1,0:T(8,128)S(1)} %collective-permute-done.11.refs_14_.refs_5_), channel_id=1, source_target_pairs={{0,1},{1,0},{2,3},{3,2},{4,5},{5,4},{6,7},{7,6},{8,9},{9,8},{10,11... | collective-permute-start | bytes 786440 | tf_op jit(solution)/shard_map/ppermute | solution.py:574
  40.0 4.5 %collective-permute-start.21 = (f32[128,512]{1,0:T(8,128)S(1)}, f32[128,512]{1,0:T(8,128)}, u32[]{:S(2)}, u32[]{:S(2)}) collective-permute-start(f32[128,512]{1,0:T(8,128)S(1)} %collective-permute-done.13.refs_16_.refs_7_), channel_id=1, source_target_pairs={{0,1},{1,0},{2,3},{3,2},{4,5},{5,4},{6,7},{7,6},{8,9},{9,8},{10,11... | collective-permute-start | bytes 786440 | tf_op jit(solution)/shard_map/ppermute | solution.py:574
  74.5 12.2 %all-to-all-start.1 = ((f32[16,16,128]{2,1,0:T(8,128)}), f32[16,16,128]{2,1,0:T(8,128)S(1)}, u32[]{:S(2)}, u32[]{:S(2)}) async-start(f32[16,16,128]{2,1,0:T(8,128)} %get-tuple-element.58), calls=%async_computation.1 | async-start | bytes 262144 | tf_op jit(solution)/shard_map/all_to_all | solution.py:537
  91.4 9.6 %all-to-all-start.2 = ((f32[8,8,128]{2,1,0:T(8,128)}), f32[8,8,128]{2,1,0:T(8,128)S(1)}, u32[]{:S(2)}, u32[]{:S(2)}) async-start(f32[8,8,128]{2,1,0:T(8,128)} %get-tuple-element.59), calls=%async_computation.2 | async-start | bytes 65536 | tf_op jit(solution)/shard_map/all_to_all | solution.py:537
  104.7 17.3 %collective-permute-start.22 = (f32[1,2048]{1,0:T(1,128)S(1)}, f32[1,2048]{1,0:T(1,128)S(1)}, u32[]{:S(2)}, u32[]{:S(2)}) collective-permute-start(f32[1,2048]{1,0:T(1,128)S(1)} %get-tuple-element.61), channel_id=1, source_target_pairs={{0,1},{1,0},{2,3},{3,2},{4,5},{5,4},{6,7},{7,6},{8,9},{9,8},{10,11... | collective-permute-start | bytes 24584 | tf_op jit(solution)/shard_map/ppermute | solution.py:590
  112.8 9.7 %collective-permute-start.23 = (f32[128,512]{1,0:T(8,128)S(1)}, f32[128,512]{1,0:T(8,128)S(1)}, u32[]{:S(2)}, u32[]{:S(2)}) collective-permute-start(f32[128,512]{1,0:T(8,128)S(1)} %get-tuple-element.65), channel_id=1, source_target_pairs={{0,1},{1,0},{2,3},{3,2},{4,5},{5,4},{6,7},{7,6},{8,9},{9,8},{10,11... | collective-permute-start | bytes 786440 | tf_op jit(solution)/shard_map/ppermute | solution.py:593
  113.4 9.2 %collective-permute-start.24 = (f32[128,512]{1,0:T(8,128)S(1)}, f32[128,512]{1,0:T(8,128)S(1)}, u32[]{:S(2)}, u32[]{:S(2)}) collective-permute-start(f32[128,512]{1,0:T(8,128)S(1)} %get-tuple-element.67), channel_id=1, source_target_pairs={{0,1},{1,0},{2,3},{3,2},{4,5},{5,4},{6,7},{7,6},{8,9},{9,8},{10,11... | collective-permute-start | bytes 786440 | tf_op jit(solution)/shard_map/ppermute | solution.py:593
  113.5 9.5 %collective-permute-start.25 = (f32[128,512]{1,0:T(8,128)S(1)}, f32[128,512]{1,0:T(8,128)S(1)}, u32[]{:S(2)}, u32[]{:S(2)}) collective-permute-start(f32[128,512]{1,0:T(8,128)S(1)} %get-tuple-element.69), channel_id=1, source_target_pairs={{0,1},{1,0},{2,3},{3,2},{4,5},{5,4},{6,7},{7,6},{8,9},{9,8},{10,11... | collective-permute-start | bytes 786440 | tf_op jit(solution)/shard_map/ppermute | solution.py:593
  122.1 1.8 %collective-permute-start.27 = (f32[128,512]{1,0:T(8,128)S(1)}, f32[128,512]{1,0:T(8,128)S(1)}, u32[]{:S(2)}, u32[]{:S(2)}) collective-permute-start(f32[128,512]{1,0:T(8,128)S(1)} %get-tuple-element.73), channel_id=1, source_target_pairs={{0,1},{1,0},{2,3},{3,2},{4,5},{5,4},{6,7},{7,6},{8,9},{9,8},{10,11... | collective-permute-start | bytes 786440 | tf_op jit(solution)/shard_map/ppermute | solution.py:593
  122.6 2.0 %collective-permute-start.29 = (f32[128,512]{1,0:T(8,128)S(1)}, f32[128,512]{1,0:T(8,128)S(1)}, u32[]{:S(2)}, u32[]{:S(2)}) collective-permute-start(f32[128,512]{1,0:T(8,128)S(1)} %get-tuple-element.77), channel_id=1, source_target_pairs={{0,1},{1,0},{2,3},{3,2},{4,5},{5,4},{6,7},{7,6},{8,9},{9,8},{10,11... | collective-permute-start | bytes 786440 | tf_op jit(solution)/shard_map/ppermute | solution.py:593
  123.0 2.0 %collective-permute-start.30 = (f32[128,512]{1,0:T(8,128)S(1)}, f32[128,512]{1,0:T(8,128)S(1)}, u32[]{:S(2)}, u32[]{:S(2)}) collective-permute-start(f32[128,512]{1,0:T(8,128)S(1)} %get-tuple-element.79), channel_id=1, source_target_pairs={{0,1},{1,0},{2,3},{3,2},{4,5},{5,4},{6,7},{7,6},{8,9},{9,8},{10,11... | collective-permute-start | bytes 786440 | tf_op jit(solution)/shard_map/ppermute | solution.py:593
  123.5 5.5 %collective-permute-start.45 = (f32[4,128]{1,0:T(4,128)S(1)}, f32[4,128]{1,0:T(4,128)S(1)}, u32[]{:S(2)}, u32[]{:S(2)}) collective-permute-start(f32[4,128]{1,0:T(4,128)S(1)} %fusion.9), channel_id=1, source_target_pairs={{0,1},{1,0},{2,3},{3,2},{4,5},{5,4},{6,7},{7,6},{8,9},{9,8},{10,11... | collective-permute-start | bytes 6152 | tf_op jit(solution)/shard_map/ppermute | solution.py:607
  125.7 11.0 %all-to-all-start.3 = ((f32[8,16,128]{2,1,0:T(8,128)}), f32[8,16,128]{2,1,0:T(8,128)S(1)}, u32[]{:S(2)}, u32[]{:S(2)}) async-start(f32[8,16,128]{2,1,0:T(8,128)} %broadcast_in_dim.8), calls=%async_computation.3 | async-start | bytes 131072 | tf_op jit(solution)/shard_map/all_to_all | solution.py:537
  129.7 30.0 %collective-permute-start.39 = (f32[128,512]{1,0:T(8,128)S(1)}, f32[128,512]{1,0:T(8,128)S(1)}, u32[]{:S(2)}, u32[]{:S(2)}) collective-permute-start(f32[128,512]{1,0:T(8,128)S(1)} %add.339), channel_id=1, source_target_pairs={{0,8},{8,16},{16,24},{24,0},{1,9},{9,17},{17,25},{25,1},{2,10},{10... | collective-permute-start | bytes 786440 | tf_op jit(solution)/shard_map/ppermute | solution.py:562
  131.6 30.7 %collective-permute-start.40 = (f32[128,512]{1,0:T(8,128)S(1)}, f32[128,512]{1,0:T(8,128)S(1)}, u32[]{:S(2)}, u32[]{:S(2)}) collective-permute-start(f32[128,512]{1,0:T(8,128)S(1)} %add.341), channel_id=1, source_target_pairs={{0,24},{8,0},{16,8},{24,16},{1,25},{9,1},{17,9},{25,17},{2,26},{10... | collective-permute-start | bytes 786440 | tf_op jit(solution)/shard_map/ppermute | solution.py:562
  132.9 22.7 %collective-permute-start.42 = (f32[128,512]{1,0:T(8,128)S(1)}, f32[128,512]{1,0:T(8,128)S(1)}, u32[]{:S(2)}, u32[]{:S(2)}) collective-permute-start(f32[128,512]{1,0:T(8,128)S(1)} %add.340), channel_id=1, source_target_pairs={{32,64},{64,32},{0,96},{96,0},{33,65},{65,33},{1,97},{97,1},{34,66... | collective-permute-start | bytes 786440 | tf_op jit(solution)/shard_map/ppermute | solution.py:561
  151.1 3.8 %collective-permute-start.46 = (f32[2,4,128]{2,1,0:T(4,128)S(1)}, f32[2,4,128]{2,1,0:T(4,128)S(1)}, u32[]{:S(2)}, u32[]{:S(2)}) collective-permute-start(f32[2,4,128]{2,1,0:T(4,128)S(1)} %dynamic-slice_bitcast_fusion), channel_id=1, source_target_pairs={{0,32},{32,0},{64,96},{96,64},{1,33},{33,1},{65,97},{97,65},{2,34}... | collective-permute-start | bytes 12296 | tf_op jit(solution)/shard_map/ppermute | solution.py:611
  151.2 7.7 %collective-permute-start.35 = (f32[136,512]{1,0:T(8,128)S(1)}, f32[136,512]{1,0:T(8,128)S(1)}, u32[]{:S(2)}, u32[]{:S(2)}) collective-permute-start(f32[136,512]{1,0:T(8,128)S(1)} %get-tuple-element.88), channel_id=1, source_target_pairs={{0,32},{32,0},{64,96},{96,64},{1,33},{33,1},{65,97},{97,65},{2,34}... | collective-permute-start | bytes 835592 | tf_op jit(solution)/shard_map/ppermute | solution.py:561
  154.9 12.8 %collective-permute-start.32 = (f32[136,512]{1,0:T(8,128)S(1)}, f32[136,512]{1,0:T(8,128)S(1)}, u32[]{:S(2)}, u32[]{:S(2)}) collective-permute-start(f32[136,512]{1,0:T(8,128)S(1)} %get-tuple-element.84), channel_id=1, source_target_pairs={{0,2},{2,4},{4,6},{6,0},{1,3},{3,5},{5,7},{7,1},{8,10},{10,12},{12... | collective-permute-start | bytes 835592 | tf_op jit(solution)/shard_map/ppermute | solution.py:562
  155.6 13.0 %collective-permute-start.33 = (f32[136,512]{1,0:T(8,128)S(1)}, f32[136,512]{1,0:T(8,128)S(1)}, u32[]{:S(2)}, u32[]{:S(2)}) collective-permute-start(f32[136,512]{1,0:T(8,128)S(1)} %get-tuple-element.85), channel_id=1, source_target_pairs={{0,6},{2,0},{4,2},{6,4},{1,7},{3,1},{5,3},{7,5},{8,14},{10,8},{12,... | collective-permute-start | bytes 835592 | tf_op jit(solution)/shard_map/ppermute | solution.py:562
  158.9 7.6 %collective-permute-start.43 = (f32[128,512]{1,0:T(8,128)S(1)}, f32[128,512]{1,0:T(8,128)S(1)}, u32[]{:S(2)}, u32[]{:S(2)}) collective-permute-start(f32[128,512]{1,0:T(8,128)S(1)} %add.353), channel_id=1, source_target_pairs={{0,8},{8,16},{16,24},{24,0},{1,9},{9,17},{17,25},{25,1},{2,10},{10... | collective-permute-start | bytes 786440 | tf_op jit(solution)/shard_map/ppermute | solution.py:563
  159.6 12.1 %collective-permute-start.38 = (f32[128,512]{1,0:T(8,128)S(1)}, f32[128,512]{1,0:T(8,128)S(1)}, u32[]{:S(2)}, u32[]{:S(2)}) collective-permute-start(f32[128,512]{1,0:T(8,128)S(1)} %add.337), channel_id=1, source_target_pairs={{0,24},{8,0},{16,8},{24,16},{1,25},{9,1},{17,9},{25,17},{2,26},{10... | collective-permute-start | bytes 786440 | tf_op jit(solution)/shard_map/ppermute | solution.py:564
  162.3 7.8 %collective-permute-start.36 = (f32[136,512]{1,0:T(8,128)S(1)}, f32[136,512]{1,0:T(8,128)S(1)}, u32[]{:S(2)}, u32[]{:S(2)}) collective-permute-start(f32[136,512]{1,0:T(8,128)S(1)} %add.346), channel_id=1, source_target_pairs={{0,2},{2,4},{4,6},{6,0},{1,3},{3,5},{5,7},{7,1},{8,10},{10,12},{12... | collective-permute-start | bytes 835592 | tf_op jit(solution)/shard_map/ppermute | solution.py:563
  166.5 10.5 %collective-permute-start.31 = (f32[136,512]{1,0:T(8,128)S(1)}, f32[136,512]{1,0:T(8,128)S(1)}, u32[]{:S(2)}, u32[]{:S(2)}) collective-permute-start(f32[136,512]{1,0:T(8,128)S(1)} %get-tuple-element.82), channel_id=1, source_target_pairs={{0,6},{2,0},{4,2},{6,4},{1,7},{3,1},{5,3},{7,5},{8,14},{10,8},{12,... | collective-permute-start | bytes 835592 | tf_op jit(solution)/shard_map/ppermute | solution.py:564
  167.8 7.7 %collective-permute-start.41 = (f32[128,512]{1,0:T(8,128)S(1)}, f32[128,512]{1,0:T(8,128)S(1)}, u32[]{:S(2)}, u32[]{:S(2)}) collective-permute-start(f32[128,512]{1,0:T(8,128)S(1)} %add_add_fusion.2), channel_id=1, source_target_pairs={{32,64},{64,32},{0,96},{96,0},{33,65},{65,33},{1,97},{97,1},{34,66... | collective-permute-start | bytes 786440 | tf_op jit(solution)/shard_map/ppermute | solution.py:565
  168.6 7.6 %collective-permute-start.44 = (f32[128,512]{1,0:T(8,128)S(1)}, f32[128,512]{1,0:T(8,128)S(1)}, u32[]{:S(2)}, u32[]{:S(2)}) collective-permute-start(f32[128,512]{1,0:T(8,128)S(1)} %add.354), channel_id=1, source_target_pairs={{0,8},{8,16},{16,24},{24,0},{1,9},{9,17},{17,25},{25,1},{2,10},{10... | collective-permute-start | bytes 786440 | tf_op jit(solution)/shard_map/ppermute | solution.py:565
  170.0 7.0 %collective-permute-start.34 = (f32[136,512]{1,0:T(8,128)S(1)}, f32[136,512]{1,0:T(8,128)S(1)}, u32[]{:S(2)}, u32[]{:S(2)}) collective-permute-start(f32[136,512]{1,0:T(8,128)S(1)} %add_add_fusion.1), channel_id=1, source_target_pairs={{0,32},{32,0},{64,96},{96,64},{1,33},{33,1},{65,97},{97,65},{2,34}... | collective-permute-start | bytes 835592 | tf_op jit(solution)/shard_map/ppermute | solution.py:565
  171.7 7.8 %collective-permute-start.37 = (f32[136,512]{1,0:T(8,128)S(1)}, f32[136,512]{1,0:T(8,128)S(1)}, u32[]{:S(2)}, u32[]{:S(2)}) collective-permute-start(f32[136,512]{1,0:T(8,128)S(1)} %add.347), channel_id=1, source_target_pairs={{0,2},{2,4},{4,6},{6,0},{1,3},{3,5},{5,7},{7,1},{8,10},{10,12},{12... | collective-permute-start | bytes 835592 | tf_op jit(solution)/shard_map/ppermute | solution.py:565
  (19 other events, 229.2 us)

commit v2 on v1

--- a/solution.py
+++ b/solution.py
@@ -39,7 +39,7 @@
 SCALE = LOG2E / EPSILON
 BLOCK = 256
 WIDE = 512
-TALL = 512
+TALL = 1024
 CHUNK = 64
 VMEM_LIMIT = 32 * 1024 * 1024
 

time: 181 us -> 180 us (level)
  no operation moved by 1% of the time
where the time goes in v2:
time: 180 us
  Pallas kernels  57.1 us (32%)
  starting transfers between devices  55.3 us (31%)
  waiting for transfers between devices  50 us (28%)
  blocking collectives  10.4 us (6%)
  other arithmetic  3.64 us (2%)
  local copies, waits for them, and re-layouts  2.37 us (1%)
    pallas_call x7, Pallas kernels, call(): pl.pallas_call(kernel, in_specs=[smem] * len(scalars) + [anywhere] * len(...  57.1 us
    all_to_all x3, waiting for transfers between devices, exchanged(): lax.all_to_all(mine, ALL, 0, 0, axis_index_groups=groups, tiled=True)  14.3 us
    all_to_all x3, starting transfers between devices, exchanged(): lax.all_to_all(mine, ALL, 0, 0, axis_index_groups=groups, tiled=True)  11.2 us
    all_to_all x1, blocking collectives, exchanged(): lax.all_to_all(mine, ALL, 0, 0, axis_index_groups=groups, tiled=True)  10.4 us
    ppermute x2, starting transfers between devices, spread(): above = lax.ppermute(own, ring, DOWN)  6.95 us
    ppermute x2, waiting for transfers between devices, spread(): over_far = lax.ppermute(far, 'y', across)  6.91 us
    ppermute x2, waiting for transfers between devices, spread(): far = lax.ppermute(below, ring, UP)  6.75 us
    ppermute x2, starting transfers between devices, spread(): over_above = lax.ppermute(over, ring, DOWN)  5.29 us
  transfers between devices with their start and end apart: 50, of which 22 were waited for; matrix products, arithmetic and copies ran while one was open for 2% of the time, Pallas kernels for 17%

profile of v2, /device:TPU:0, one launch (start us, length us, event | category | flops | bytes accessed | tf_op | source)
XLA Modules:
  0.0 180.1 jit_solution(11862700882275583560)
XLA Ops:
  0.6 2.9 %collective-permute-start.1 = (f32[128,512]{1,0:T(8,128)}, f32[128,512]{1,0:T(8,128)S(1)}, u32[]{:S(2)}, u32[]{:S(2)}) collective-permute-start(f32[128,512]{1,0:T(8,128)} %refs_1_.1), channel_id=1, source_target_pairs={{0,6},{2,0},{4,2},{6,4},{1,7},{3,1},{5,3},{7,5},{8,14},{10,8},{12,... | collective-permute-start | bytes 786440 | tf_op jit(solution)/shard_map/ppermute | solution.py:549
  3.5 1.6 collective-permute-start.2
  5.1 2.2 %collective-permute-start.9 = (f32[128,512]{1,0:T(8,128)}, f32[128,512]{1,0:T(8,128)S(1)}, u32[]{:S(2)}, u32[]{:S(2)}) collective-permute-start(f32[128,512]{1,0:T(8,128)} %refs_0_.1), channel_id=1, source_target_pairs={{32,64},{64,32},{0,96},{96,0},{33,65},{65,33},{1,97},{97,1},{34,66... | collective-permute-start | bytes 786440 | tf_op jit(solution)/shard_map/ppermute | solution.py:550
  7.3 2.1 %collective-permute-done.1.refs_3_ = f32[128,512]{1,0:T(8,128)S(1)} collective-permute-done((f32[128,512]{1,0:T(8,128)}, f32[128,512]{1,0:T(8,128)S(1)}, u32[]{:S(2)}, u32[]{:S(2)}) %collective-permute-start.1) | collective-permute-done | bytes 262176 | tf_op jit(solution)/shard_map/ppermute | solution.py:549
  9.4 4.0 %collective-permute-start.8 = (f32[128,512]{1,0:T(8,128)}, f32[128,512]{1,0:T(8,128)S(1)}, u32[]{:S(2)}, u32[]{:S(2)}) collective-permute-start(f32[128,512]{1,0:T(8,128)} %refs_0_.1), channel_id=1, source_target_pairs={{0,24},{8,0},{16,8},{24,16},{1,25},{9,1},{17,9},{25,17},{2,26},{10... | collective-permute-start | bytes 786440 | tf_op jit(solution)/shard_map/ppermute | solution.py:549
  13.5 1.2 collective-permute-start.7
  14.7 3.2 %collective-permute-start.5 = (f32[128,512]{1,0:T(8,128)S(1)}, f32[128,512]{1,0:T(8,128)}, u32[]{:S(2)}, u32[]{:S(2)}) collective-permute-start(f32[128,512]{1,0:T(8,128)S(1)} %collective-permute-done.2.refs_4_), channel_id=1, source_target_pairs={{0,6},{2,0},{4,2},{6,4},{1,7},{3,1},{5,3},{7,5},{8,14},{10,8},{12,... | collective-permute-start | bytes 786440 | tf_op jit(solution)/shard_map/ppermute | solution.py:553
  18.5 3.6 %collective-permute-done.7.refs_10_.refs_1_ = f32[128,512]{1,0:T(8,128)S(1)} collective-permute-done((f32[128,512]{1,0:T(8,128)}, f32[128,512]{1,0:T(8,128)S(1)}, u32[]{:S(2)}, u32[]{:S(2)}) %collective-permute-start.7) | collective-permute-done | bytes 262176 | tf_op jit(solution)/shard_map/ppermute | solution.py:548
  22.1 3.1 %collective-permute-done.3.refs_5_ = f32[128,512]{1,0:T(8,128)} collective-permute-done((f32[128,512]{1,0:T(8,128)S(1)}, f32[128,512]{1,0:T(8,128)}, u32[]{:S(2)}, u32[]{:S(2)}) %collective-permute-start.3) | collective-permute-done | bytes 262176 | tf_op jit(solution)/shard_map/ppermute | solution.py:551
  25.2 2.1 %collective-permute-start.12 = (f32[128,512]{1,0:T(8,128)S(1)}, f32[128,512]{1,0:T(8,128)S(1)}, u32[]{:S(2)}, u32[]{:S(2)}) collective-permute-start(f32[128,512]{1,0:T(8,128)S(1)} %collective-permute-done.9.refs_12_.refs_3_), channel_id=1, source_target_pairs={{0,24},{8,0},{16,8},{24,16},{1,25},{9,1},{17,9},{25,17},{2,26},{10... | collective-permute-start | bytes 786440 | tf_op jit(solution)/shard_map/ppermute | solution.py:553
  27.3 0.8 collective-permute-done.4.refs_6_
  28.1 0.7 copy-done.16
  28.8 3.6 %collective-permute-done.10.refs_13_.refs_4_ = f32[128,512]{1,0:T(8,128)S(1)} collective-permute-done((f32[128,512]{1,0:T(8,128)S(1)}, f32[128,512]{1,0:T(8,128)S(1)}, u32[]{:S(2)}, u32[]{:S(2)}) %collective-permute-start.10) | collective-permute-done | bytes 262176 | tf_op jit(solution)/shard_map/ppermute | solution.py:551
  32.4 3.0 %collective-permute-start.13 = (f32[128,512]{1,0:T(8,128)S(1)}, f32[128,512]{1,0:T(8,128)S(1)}, u32[]{:S(2)}, u32[]{:S(2)}) collective-permute-start(f32[128,512]{1,0:T(8,128)S(1)} %collective-permute-done.10.refs_13_.refs_4_), channel_id=1, source_target_pairs={{32,64},{64,32},{0,96},{96,0},{33,65},{65,33},{1,97},{97,1},{34,66... | collective-permute-start | bytes 786440 | tf_op jit(solution)/shard_map/ppermute | solution.py:554
  35.5 1.3 collective-permute-start.6
  37.3 2.7 %collective-permute-done.13.refs_16_.refs_7_ = f32[128,512]{1,0:T(8,128)S(1)} collective-permute-done((f32[128,512]{1,0:T(8,128)S(1)}, f32[128,512]{1,0:T(8,128)S(1)}, u32[]{:S(2)}, u32[]{:S(2)}) %collective-permute-start.13) | collective-permute-done | bytes 262176 | tf_op jit(solution)/shard_map/ppermute | solution.py:554
  40.3 4.2 %collective-permute-done.6.refs_8_ = f32[128,512]{1,0:T(8,128)} collective-permute-done((f32[128,512]{1,0:T(8,128)}, f32[128,512]{1,0:T(8,128)}, u32[]{:S(2)}, u32[]{:S(2)}) %collective-permute-start.6) | collective-permute-done | bytes 262176 | tf_op jit(solution)/shard_map/ppermute | solution.py:554
  45.3 13.7 %shard_map.57 = (f32[512,1024]{1,0:T(8,128)}, f32[1024,2048]{1,0:T(8,128)S(1)}, f32[8,8,128]{2,1,0:T(8,128)S(1)}, f32[1,1024]{1,0:T(1,128)S(1)}, f32[1,2048]{1,0:T(1,128)S(1)}) custom-call(s32[24]{0:T(128)S(1)} %stack.117.refs_0_, f32[128,512]{1,0:T(8,128)} %refs_1_.1, f32[128,512]{1,0:T(8,128)} %copy-done.14, f32[128,512]{1,0:T(8,128)} %copy-done.13, ...), custom_call_target="tpu_custom_call" | custom-call | flops 6442450944 | bytes 16822272 | tf_op jit(solution)/shard_map/pallas_call | solution.py:78
  59.0 10.4 %all_to_all.20 = f32[8,8,128]{2,1,0:T(8,128)S(1)} all-to-all(f32[8,8,128]{2,1,0:T(8,128)S(1)} %get-tuple-element.54), channel_id=1, replica_groups={{0,2,4,6,32,34,36,38},{1,3,5,7,33,35,37,39},{8,10,12,14,40,42,44,46},{9..., dimensions={0} | all-to-all | bytes 65536 | tf_op jit(solution)/shard_map/all_to_all | solution.py:537
  69.4 5.1 %shard_map.58 = (bf16[8,1024,256]{2,1,0:T(8,128)(2,1)}, bf16[8,1024,256]{2,1,0:T(8,128)(2,1)}, f32[1,2048]{1,0:T(1,128)S(1)}, f32[16,16,128]{2,1,0:T(8,128)}, f32[1,1024]{1,0:T(1,128)S(1)}) custom-call(f32[1024,2048]{1,0:T(8,128)S(1)} %get-tuple-element.53.s_ref, f32[8,1024]{1,0:T(8,128)S(1)} %bitcast.60), custom_call_target="tpu_custom_call" | custom-call | flops 8388608 | bytes 16953344 | tf_op jit(solution)/shard_map/pallas_call | solution.py:78
  74.5 4.5 %all-to-all-start.1 = ((f32[16,16,128]{2,1,0:T(8,128)}), f32[16,16,128]{2,1,0:T(8,128)S(1)}, u32[]{:S(2)}, u32[]{:S(2)}) async-start(f32[16,16,128]{2,1,0:T(8,128)} %get-tuple-element.58), calls=%async_computation.1 | async-start | bytes 262144 | tf_op jit(solution)/shard_map/all_to_all | solution.py:537
  79.0 7.7 %all-to-all-done.1 = f32[16,16,128]{2,1,0:T(8,128)S(1)} async-done(((f32[16,16,128]{2,1,0:T(8,128)}), f32[16,16,128]{2,1,0:T(8,128)S(1)}, u32[]{:S(2)}, u32[]{:S(2)}) %all-to-all-start.1) | async-done | bytes 131104 | tf_op jit(solution)/shard_map/all_to_all | solution.py:537
  86.8 4.6 %shard_map.59 = (f32[8,8,128]{2,1,0:T(8,128)}, f32[1,2048]{1,0:T(1,128)S(1)}, f32[1,2048]{1,0:T(1,128)S(1)}) custom-call(bf16[8,1024,256]{2,1,0:T(8,128)(2,1)} %get-tuple-element.55.high.high_from, bf16[8,1024,256]{2,1,0:T(8,128)(2,1)} %get-tuple-element.56.low.low_from, f32[1,2048]{1,0:T(1,128)S(1)} %get-tuple-element.57.top_ref, f32[16,2048]{1,0:T(8,128)S(1)} %bitcast.59), custom_call_target="tpu_custom_call" | custom-call | flops 8388608 | bytes 8577024 | tf_op jit(solution)/shard_map/pallas_call | solution.py:78
  91.4 3.4 %all-to-all-start.2 = ((f32[8,8,128]{2,1,0:T(8,128)}), f32[8,8,128]{2,1,0:T(8,128)S(1)}, u32[]{:S(2)}, u32[]{:S(2)}) async-start(f32[8,8,128]{2,1,0:T(8,128)} %get-tuple-element.59), calls=%async_computation.2 | async-start | bytes 65536 | tf_op jit(solution)/shard_map/all_to_all | solution.py:537
  95.0 6.0 %all-to-all-done.2 = f32[8,8,128]{2,1,0:T(8,128)S(1)} async-done(((f32[8,8,128]{2,1,0:T(8,128)}), f32[8,8,128]{2,1,0:T(8,128)S(1)}, u32[]{:S(2)}, u32[]{:S(2)}) %all-to-all-start.2) | async-done | bytes 32800 | tf_op jit(solution)/shard_map/all_to_all | solution.py:537
  101.0 3.7 %shard_map.60 = (f32[1,2048]{1,0:T(1,128)S(1)}, f32[1,1024]{1,0:T(1,128)S(1)}) custom-call(bf16[8,1024,256]{2,1,0:T(8,128)(2,1)} %get-tuple-element.55.high.high_from, bf16[8,1024,256]{2,1,0:T(8,128)(2,1)} %get-tuple-element.56.low.low_from, f32[8,1024]{1,0:T(8,128)S(1)} %bitcast.61, f32[1,2048]{1,0:T(1,128)S(1)} %get-tuple-element.60.t_ref.refs_17_), custom_call_target="tpu_custom_call" | custom-call | flops 8388608 | bytes 8441856 | tf_op jit(solution)/shard_map/pallas_call | solution.py:78
  104.8 8.0 %shard_map.62 = (f32[128,512]{1,0:T(8,128)S(1)}, f32[128,512]{1,0:T(8,128)S(1)}, f32[128,512]{1,0:T(8,128)S(1)}, f32[128,512]{1,0:T(8,128)S(1)}, f32[128,512]{1,...) custom-call(s32[17]{0:T(128)S(1)} %get-tuple-element.106.seats, ...), custom_call_target="tpu_custom_call" | custom-call | flops 3221225472 | bytes 12595200 | tf_op jit(solution)/shard_map/pallas_call | solution.py:78
  113.9 8.0 %shard_map.61 = (f32[128,512]{1,0:T(8,128)S(1)}, f32[128,512]{1,0:T(8,128)S(1)}, f32[128,512]{1,0:T(8,128)S(1)}, f32[128,512]{1,0:T(8,128)S(1)}, f32[128,512]{1,...) custom-call(s32[17]{0:T(128)S(1)} %get-tuple-element.107.seats, ...), custom_call_target="tpu_custom_call" | custom-call | flops 3221225472 | bytes 12595200 | tf_op jit(solution)/shard_map/pallas_call | solution.py:78
  125.7 3.4 %all-to-all-start.3 = ((f32[8,16,128]{2,1,0:T(8,128)}), f32[8,16,128]{2,1,0:T(8,128)S(1)}, u32[]{:S(2)}, u32[]{:S(2)}) async-start(f32[8,16,128]{2,1,0:T(8,128)} %broadcast_in_dim.8), calls=%async_computation.3 | async-start | bytes 131072 | tf_op jit(solution)/shard_map/all_to_all | solution.py:537
  129.7 1.9 %collective-permute-start.39 = (f32[128,512]{1,0:T(8,128)S(1)}, f32[128,512]{1,0:T(8,128)S(1)}, u32[]{:S(2)}, u32[]{:S(2)}) collective-permute-start(f32[128,512]{1,0:T(8,128)S(1)} %add.339), channel_id=1, source_target_pairs={{0,8},{8,16},{16,24},{24,0},{1,9},{9,17},{17,25},{25,1},{2,10},{10... | collective-permute-start | bytes 786440 | tf_op jit(solution)/shard_map/ppermute | solution.py:562
  131.6 1.3 collective-permute-start.40
  132.9 3.1 %collective-permute-start.42 = (f32[128,512]{1,0:T(8,128)S(1)}, f32[128,512]{1,0:T(8,128)S(1)}, u32[]{:S(2)}, u32[]{:S(2)}) collective-permute-start(f32[128,512]{1,0:T(8,128)S(1)} %add.340), channel_id=1, source_target_pairs={{32,64},{64,32},{0,96},{96,0},{33,65},{65,33},{1,97},{97,1},{34,66... | collective-permute-start | bytes 786440 | tf_op jit(solution)/shard_map/ppermute | solution.py:561
  136.7 14.0 %shard_map.63 = (f32[136,512]{1,0:T(8,128)S(1)}, f32[136,512]{1,0:T(8,128)S(1)}, f32[136,512]{1,0:T(8,128)S(1)}, f32[136,512]{1,0:T(8,128)S(1)}, f32[136,512]{1,...) custom-call(s32[24]{0:T(128)S(1)} %concatenate.11.seats, ...), custom_call_target="tpu_custom_call" | custom-call | flops 6442450944 | bytes 14893056 | tf_op jit(solution)/shard_map/pallas_call | solution.py:78
  150.8 2.0 %collective-permute-start.35 = (f32[136,512]{1,0:T(8,128)S(1)}, f32[136,512]{1,0:T(8,128)S(1)}, u32[]{:S(2)}, u32[]{:S(2)}) collective-permute-start(f32[136,512]{1,0:T(8,128)S(1)} %get-tuple-element.88), channel_id=1, source_target_pairs={{0,32},{32,0},{64,96},{96,64},{1,33},{33,1},{65,97},{97,65},{2,34}... | collective-permute-start | bytes 835592 | tf_op jit(solution)/shard_map/ppermute | solution.py:561
  152.8 1.7 collective-permute-done.46
  155.2 2.6 %collective-permute-start.33 = (f32[136,512]{1,0:T(8,128)S(1)}, f32[136,512]{1,0:T(8,128)S(1)}, u32[]{:S(2)}, u32[]{:S(2)}) collective-permute-start(f32[136,512]{1,0:T(8,128)S(1)} %get-tuple-element.85), channel_id=1, source_target_pairs={{0,6},{2,0},{4,2},{6,4},{1,7},{3,1},{5,3},{7,5},{8,14},{10,8},{12,... | collective-permute-start | bytes 835592 | tf_op jit(solution)/shard_map/ppermute | solution.py:562
  158.5 0.7 collective-permute-start.43
  159.2 2.6 %collective-permute-start.38 = (f32[128,512]{1,0:T(8,128)S(1)}, f32[128,512]{1,0:T(8,128)S(1)}, u32[]{:S(2)}, u32[]{:S(2)}) collective-permute-start(f32[128,512]{1,0:T(8,128)S(1)} %add.337), channel_id=1, source_target_pairs={{0,24},{8,0},{16,8},{24,16},{1,25},{9,1},{17,9},{25,17},{2,26},{10... | collective-permute-start | bytes 786440 | tf_op jit(solution)/shard_map/ppermute | solution.py:564
  162.6 3.5 %collective-permute-done.43 = f32[128,512]{1,0:T(8,128)S(1)} collective-permute-done((f32[128,512]{1,0:T(8,128)S(1)}, f32[128,512]{1,0:T(8,128)S(1)}, u32[]{:S(2)}, u32[]{:S(2)}) %collective-permute-start.43) | collective-permute-done | bytes 262176 | tf_op jit(solution)/shard_map/ppermute | solution.py:563
  166.1 1.2 collective-permute-start.31
  167.3 0.8 collective-permute-start.41
  168.2 1.4 collective-permute-done.36
  169.6 1.7 collective-permute-start.34
  172.0 3.0 %collective-permute-done.41 = f32[128,512]{1,0:T(8,128)S(1)} collective-permute-done((f32[128,512]{1,0:T(8,128)S(1)}, f32[128,512]{1,0:T(8,128)S(1)}, u32[]{:S(2)}, u32[]{:S(2)}) %collective-permute-start.41) | collective-permute-done | bytes 262176 | tf_op jit(solution)/shard_map/ppermute | solution.py:565
  175.0 0.8 collective-permute-done.44
  175.8 0.8 add_divide_fusion
  176.6 2.6 %collective-permute-done.37 = f32[136,512]{1,0:T(8,128)S(1)} collective-permute-done((f32[136,512]{1,0:T(8,128)S(1)}, f32[136,512]{1,0:T(8,128)S(1)}, u32[]{:S(2)}, u32[]{:S(2)}) %collective-permute-start.37) | collective-permute-done | bytes 278560 | tf_op jit(solution)/shard_map/ppermute | solution.py:565
  179.3 0.8 slice_divide_fusion
  (134 shorter events, 11.5 us)
Async XLA Ops:
  0.6 8.8 %collective-permute-start.1 = (f32[128,512]{1,0:T(8,128)}, f32[128,512]{1,0:T(8,128)S(1)}, u32[]{:S(2)}, u32[]{:S(2)}) collective-permute-start(f32[128,512]{1,0:T(8,128)} %refs_1_.1), channel_id=1, source_target_pairs={{0,6},{2,0},{4,2},{6,4},{1,7},{3,1},{5,3},{7,5},{8,14},{10,8},{12,... | collective-permute-start | bytes 786440 | tf_op jit(solution)/shard_map/ppermute | solution.py:549
  3.5 9.9 %collective-permute-start = (f32[128,512]{1,0:T(8,128)}, f32[128,512]{1,0:T(8,128)S(1)}, u32[]{:S(2)}, u32[]{:S(2)}) collective-permute-start(f32[128,512]{1,0:T(8,128)} %refs_1_.1), channel_id=1, source_target_pairs={{0,2},{2,4},{4,6},{6,0},{1,3},{3,5},{5,7},{7,1},{8,10},{10,12},{12... | collective-permute-start | bytes 786440 | tf_op jit(solution)/shard_map/ppermute | solution.py:548
  3.5 11.1 %collective-permute-start.2 = (f32[128,512]{1,0:T(8,128)}, f32[128,512]{1,0:T(8,128)S(1)}, u32[]{:S(2)}, u32[]{:S(2)}) collective-permute-start(f32[128,512]{1,0:T(8,128)} %refs_1_.1), channel_id=1, source_target_pairs={{0,32},{32,0},{64,96},{96,64},{1,33},{33,1},{65,97},{97,65},{2,34}... | collective-permute-start | bytes 786440 | tf_op jit(solution)/shard_map/ppermute | solution.py:550
  5.1 9.6 %collective-permute-start.14 = (f32[128,512]{1,0:T(8,128)}, f32[128,512]{1,0:T(8,128)S(1)}, u32[]{:S(2)}, u32[]{:S(2)}) collective-permute-start(f32[128,512]{1,0:T(8,128)} %refs_0_.1), channel_id=1, source_target_pairs={{0,1},{1,0},{2,3},{3,2},{4,5},{5,4},{6,7},{7,6},{8,9},{9,8},{10,11... | collective-permute-start | bytes 786440 | tf_op jit(solution)/shard_map/ppermute | solution.py:574
  5.1 12.8 %collective-permute-start.9 = (f32[128,512]{1,0:T(8,128)}, f32[128,512]{1,0:T(8,128)S(1)}, u32[]{:S(2)}, u32[]{:S(2)}) collective-permute-start(f32[128,512]{1,0:T(8,128)} %refs_0_.1), channel_id=1, source_target_pairs={{32,64},{64,32},{0,96},{96,0},{33,65},{65,33},{1,97},{97,1},{34,66... | collective-permute-start | bytes 786440 | tf_op jit(solution)/shard_map/ppermute | solution.py:550
  9.4 9.0 %collective-permute-start.8 = (f32[128,512]{1,0:T(8,128)}, f32[128,512]{1,0:T(8,128)S(1)}, u32[]{:S(2)}, u32[]{:S(2)}) collective-permute-start(f32[128,512]{1,0:T(8,128)} %refs_0_.1), channel_id=1, source_target_pairs={{0,24},{8,0},{16,8},{24,16},{1,25},{9,1},{17,9},{25,17},{2,26},{10... | collective-permute-start | bytes 786440 | tf_op jit(solution)/shard_map/ppermute | solution.py:549
  13.5 8.6 %collective-permute-start.7 = (f32[128,512]{1,0:T(8,128)}, f32[128,512]{1,0:T(8,128)S(1)}, u32[]{:S(2)}, u32[]{:S(2)}) collective-permute-start(f32[128,512]{1,0:T(8,128)} %refs_0_.1), channel_id=1, source_target_pairs={{0,8},{8,16},{16,24},{24,0},{1,9},{9,17},{17,25},{25,1},{2,10},{10... | collective-permute-start | bytes 786440 | tf_op jit(solution)/shard_map/ppermute | solution.py:548
  14.7 10.6 %collective-permute-start.3 = (f32[128,512]{1,0:T(8,128)S(1)}, f32[128,512]{1,0:T(8,128)}, u32[]{:S(2)}, u32[]{:S(2)}) collective-permute-start(f32[128,512]{1,0:T(8,128)S(1)} %collective-permute-done.refs_2_), channel_id=1, source_target_pairs={{0,2},{2,4},{4,6},{6,0},{1,3},{3,5},{5,7},{7,1},{8,10},{10,12},{12... | collective-permute-start | bytes 786440 | tf_op jit(solution)/shard_map/ppermute | solution.py:551
  14.7 12.6 %collective-permute-start.5 = (f32[128,512]{1,0:T(8,128)S(1)}, f32[128,512]{1,0:T(8,128)}, u32[]{:S(2)}, u32[]{:S(2)}) collective-permute-start(f32[128,512]{1,0:T(8,128)S(1)} %collective-permute-done.2.refs_4_), channel_id=1, source_target_pairs={{0,6},{2,0},{4,2},{6,4},{1,7},{3,1},{5,3},{7,5},{8,14},{10,8},{12,... | collective-permute-start | bytes 786440 | tf_op jit(solution)/shard_map/ppermute | solution.py:553
  17.9 10.2 %collective-permute-start.4 = (f32[128,512]{1,0:T(8,128)S(1)}, f32[128,512]{1,0:T(8,128)S(1)}, u32[]{:S(2)}, u32[]{:S(2)}) collective-permute-start(f32[128,512]{1,0:T(8,128)S(1)} %collective-permute-done.2.refs_4_), channel_id=1, source_target_pairs={{0,2},{2,4},{4,6},{6,0},{1,3},{3,5},{5,7},{7,1},{8,10},{10,12},{12... | collective-permute-start | bytes 786440 | tf_op jit(solution)/shard_map/ppermute | solution.py:552
  18.5 10.3 %collective-permute-start.17 = (f32[128,512]{1,0:T(8,128)S(1)}, f32[128,512]{1,0:T(8,128)S(1)}, u32[]{:S(2)}, u32[]{:S(2)}) collective-permute-start(f32[128,512]{1,0:T(8,128)S(1)} %collective-permute-done.9.refs_12_.refs_3_), channel_id=1, source_target_pairs={{0,1},{1,0},{2,3},{3,2},{4,5},{5,4},{6,7},{7,6},{8,9},{9,8},{10,11... | collective-permute-start | bytes 786440 | tf_op jit(solution)/shard_map/ppermute | solution.py:574
  22.1 10.3 %collective-permute-start.10 = (f32[128,512]{1,0:T(8,128)S(1)}, f32[128,512]{1,0:T(8,128)S(1)}, u32[]{:S(2)}, u32[]{:S(2)}) collective-permute-start(f32[128,512]{1,0:T(8,128)S(1)} %collective-permute-done.7.refs_10_.refs_1_), channel_id=1, source_target_pairs={{0,8},{8,16},{16,24},{24,0},{1,9},{9,17},{17,25},{25,1},{2,10},{10... | collective-permute-start | bytes 786440 | tf_op jit(solution)/shard_map/ppermute | solution.py:551
  25.2 10.2 %collective-permute-start.12 = (f32[128,512]{1,0:T(8,128)S(1)}, f32[128,512]{1,0:T(8,128)S(1)}, u32[]{:S(2)}, u32[]{:S(2)}) collective-permute-start(f32[128,512]{1,0:T(8,128)S(1)} %collective-permute-done.9.refs_12_.refs_3_), channel_id=1, source_target_pairs={{0,24},{8,0},{16,8},{24,16},{1,25},{9,1},{17,9},{25,17},{2,26},{10... | collective-permute-start | bytes 786440 | tf_op jit(solution)/shard_map/ppermute | solution.py:553
  27.3 8.2 %collective-permute-start.11 = (f32[128,512]{1,0:T(8,128)S(1)}, f32[128,512]{1,0:T(8,128)S(1)}, u32[]{:S(2)}, u32[]{:S(2)}) collective-permute-start(f32[128,512]{1,0:T(8,128)S(1)} %collective-permute-done.9.refs_12_.refs_3_), channel_id=1, source_target_pairs={{0,8},{8,16},{16,24},{24,0},{1,9},{9,17},{17,25},{25,1},{2,10},{10... | collective-permute-start | bytes 786440 | tf_op jit(solution)/shard_map/ppermute | solution.py:552
  28.1 8.8 %collective-permute-start.16 = (f32[128,512]{1,0:T(8,128)S(1)}, f32[128,512]{1,0:T(8,128)S(1)}, u32[]{:S(2)}, u32[]{:S(2)}) collective-permute-start(f32[128,512]{1,0:T(8,128)S(1)} %collective-permute-done.8.refs_11_.refs_2_), channel_id=1, source_target_pairs={{0,1},{1,0},{2,3},{3,2},{4,5},{5,4},{6,7},{7,6},{8,9},{9,8},{10,11... | collective-permute-start | bytes 786440 | tf_op jit(solution)/shard_map/ppermute | solution.py:574
  28.8 8.0 %collective-permute-start.15 = (f32[128,512]{1,0:T(8,128)S(1)}, f32[128,512]{1,0:T(8,128)S(1)}, u32[]{:S(2)}, u32[]{:S(2)}) collective-permute-start(f32[128,512]{1,0:T(8,128)S(1)} %collective-permute-done.7.refs_10_.refs_1_), channel_id=1, source_target_pairs={{0,1},{1,0},{2,3},{3,2},{4,5},{5,4},{6,7},{7,6},{8,9},{9,8},{10,11... | collective-permute-start | bytes 786440 | tf_op jit(solution)/shard_map/ppermute | solution.py:574
  32.4 7.6 %collective-permute-start.13 = (f32[128,512]{1,0:T(8,128)S(1)}, f32[128,512]{1,0:T(8,128)S(1)}, u32[]{:S(2)}, u32[]{:S(2)}) collective-permute-start(f32[128,512]{1,0:T(8,128)S(1)} %collective-permute-done.10.refs_13_.refs_4_), channel_id=1, source_target_pairs={{32,64},{64,32},{0,96},{96,0},{33,65},{65,33},{1,97},{97,1},{34,66... | collective-permute-start | bytes 786440 | tf_op jit(solution)/shard_map/ppermute | solution.py:554
  35.5 9.1 %collective-permute-start.18 = (f32[128,512]{1,0:T(8,128)S(1)}, f32[128,512]{1,0:T(8,128)S(1)}, u32[]{:S(2)}, u32[]{:S(2)}) collective-permute-start(f32[128,512]{1,0:T(8,128)S(1)} %collective-permute-done.10.refs_13_.refs_4_), channel_id=1, source_target_pairs={{0,1},{1,0},{2,3},{3,2},{4,5},{5,4},{6,7},{7,6},{8,9},{9,8},{10,11... | collective-permute-start | bytes 786440 | tf_op jit(solution)/shard_map/ppermute | solution.py:574
  35.5 9.0 %collective-permute-start.6 = (f32[128,512]{1,0:T(8,128)}, f32[128,512]{1,0:T(8,128)}, u32[]{:S(2)}, u32[]{:S(2)}) collective-permute-start(f32[128,512]{1,0:T(8,128)} %collective-permute-done.3.refs_5_), channel_id=1, source_target_pairs={{0,32},{32,0},{64,96},{96,64},{1,33},{33,1},{65,97},{97,65},{2,34}... | collective-permute-start | bytes 786440 | tf_op jit(solution)/shard_map/ppermute | solution.py:554
  36.8 7.7 %collective-permute-start.20 = (f32[128,512]{1,0:T(8,128)S(1)}, f32[128,512]{1,0:T(8,128)S(1)}, u32[]{:S(2)}, u32[]{:S(2)}) collective-permute-start(f32[128,512]{1,0:T(8,128)S(1)} %collective-permute-done.12.refs_15_.refs_6_), channel_id=1, source_target_pairs={{0,1},{1,0},{2,3},{3,2},{4,5},{5,4},{6,7},{7,6},{8,9},{9,8},{10,11... | collective-permute-start | bytes 786440 | tf_op jit(solution)/shard_map/ppermute | solution.py:574
  36.9 7.7 %collective-permute-start.19 = (f32[128,512]{1,0:T(8,128)S(1)}, f32[128,512]{1,0:T(8,128)}, u32[]{:S(2)}, u32[]{:S(2)}) collective-permute-start(f32[128,512]{1,0:T(8,128)S(1)} %collective-permute-done.11.refs_14_.refs_5_), channel_id=1, source_target_pairs={{0,1},{1,0},{2,3},{3,2},{4,5},{5,4},{6,7},{7,6},{8,9},{9,8},{10,11... | collective-permute-start | bytes 786440 | tf_op jit(solution)/shard_map/ppermute | solution.py:574
  40.0 4.5 %collective-permute-start.21 = (f32[128,512]{1,0:T(8,128)S(1)}, f32[128,512]{1,0:T(8,128)}, u32[]{:S(2)}, u32[]{:S(2)}) collective-permute-start(f32[128,512]{1,0:T(8,128)S(1)} %collective-permute-done.13.refs_16_.refs_7_), channel_id=1, source_target_pairs={{0,1},{1,0},{2,3},{3,2},{4,5},{5,4},{6,7},{7,6},{8,9},{9,8},{10,11... | collective-permute-start | bytes 786440 | tf_op jit(solution)/shard_map/ppermute | solution.py:574
  74.5 12.2 %all-to-all-start.1 = ((f32[16,16,128]{2,1,0:T(8,128)}), f32[16,16,128]{2,1,0:T(8,128)S(1)}, u32[]{:S(2)}, u32[]{:S(2)}) async-start(f32[16,16,128]{2,1,0:T(8,128)} %get-tuple-element.58), calls=%async_computation.1 | async-start | bytes 262144 | tf_op jit(solution)/shard_map/all_to_all | solution.py:537
  91.4 9.6 %all-to-all-start.2 = ((f32[8,8,128]{2,1,0:T(8,128)}), f32[8,8,128]{2,1,0:T(8,128)S(1)}, u32[]{:S(2)}, u32[]{:S(2)}) async-start(f32[8,8,128]{2,1,0:T(8,128)} %get-tuple-element.59), calls=%async_computation.2 | async-start | bytes 65536 | tf_op jit(solution)/shard_map/all_to_all | solution.py:537
  104.7 17.3 %collective-permute-start.22 = (f32[1,2048]{1,0:T(1,128)S(1)}, f32[1,2048]{1,0:T(1,128)S(1)}, u32[]{:S(2)}, u32[]{:S(2)}) collective-permute-start(f32[1,2048]{1,0:T(1,128)S(1)} %get-tuple-element.61), channel_id=1, source_target_pairs={{0,1},{1,0},{2,3},{3,2},{4,5},{5,4},{6,7},{7,6},{8,9},{9,8},{10,11... | collective-permute-start | bytes 24584 | tf_op jit(solution)/shard_map/ppermute | solution.py:590
  112.8 9.7 %collective-permute-start.23 = (f32[128,512]{1,0:T(8,128)S(1)}, f32[128,512]{1,0:T(8,128)S(1)}, u32[]{:S(2)}, u32[]{:S(2)}) collective-permute-start(f32[128,512]{1,0:T(8,128)S(1)} %get-tuple-element.65), channel_id=1, source_target_pairs={{0,1},{1,0},{2,3},{3,2},{4,5},{5,4},{6,7},{7,6},{8,9},{9,8},{10,11... | collective-permute-start | bytes 786440 | tf_op jit(solution)/shard_map/ppermute | solution.py:593
  113.4 9.2 %collective-permute-start.24 = (f32[128,512]{1,0:T(8,128)S(1)}, f32[128,512]{1,0:T(8,128)S(1)}, u32[]{:S(2)}, u32[]{:S(2)}) collective-permute-start(f32[128,512]{1,0:T(8,128)S(1)} %get-tuple-element.67), channel_id=1, source_target_pairs={{0,1},{1,0},{2,3},{3,2},{4,5},{5,4},{6,7},{7,6},{8,9},{9,8},{10,11... | collective-permute-start | bytes 786440 | tf_op jit(solution)/shard_map/ppermute | solution.py:593
  113.5 9.5 %collective-permute-start.25 = (f32[128,512]{1,0:T(8,128)S(1)}, f32[128,512]{1,0:T(8,128)S(1)}, u32[]{:S(2)}, u32[]{:S(2)}) collective-permute-start(f32[128,512]{1,0:T(8,128)S(1)} %get-tuple-element.69), channel_id=1, source_target_pairs={{0,1},{1,0},{2,3},{3,2},{4,5},{5,4},{6,7},{7,6},{8,9},{9,8},{10,11... | collective-permute-start | bytes 786440 | tf_op jit(solution)/shard_map/ppermute | solution.py:593
  122.1 1.8 %collective-permute-start.27 = (f32[128,512]{1,0:T(8,128)S(1)}, f32[128,512]{1,0:T(8,128)S(1)}, u32[]{:S(2)}, u32[]{:S(2)}) collective-permute-start(f32[128,512]{1,0:T(8,128)S(1)} %get-tuple-element.73), channel_id=1, source_target_pairs={{0,1},{1,0},{2,3},{3,2},{4,5},{5,4},{6,7},{7,6},{8,9},{9,8},{10,11... | collective-permute-start | bytes 786440 | tf_op jit(solution)/shard_map/ppermute | solution.py:593
  122.6 2.0 %collective-permute-start.29 = (f32[128,512]{1,0:T(8,128)S(1)}, f32[128,512]{1,0:T(8,128)S(1)}, u32[]{:S(2)}, u32[]{:S(2)}) collective-permute-start(f32[128,512]{1,0:T(8,128)S(1)} %get-tuple-element.77), channel_id=1, source_target_pairs={{0,1},{1,0},{2,3},{3,2},{4,5},{5,4},{6,7},{7,6},{8,9},{9,8},{10,11... | collective-permute-start | bytes 786440 | tf_op jit(solution)/shard_map/ppermute | solution.py:593
  123.0 2.0 %collective-permute-start.30 = (f32[128,512]{1,0:T(8,128)S(1)}, f32[128,512]{1,0:T(8,128)S(1)}, u32[]{:S(2)}, u32[]{:S(2)}) collective-permute-start(f32[128,512]{1,0:T(8,128)S(1)} %get-tuple-element.79), channel_id=1, source_target_pairs={{0,1},{1,0},{2,3},{3,2},{4,5},{5,4},{6,7},{7,6},{8,9},{9,8},{10,11... | collective-permute-start | bytes 786440 | tf_op jit(solution)/shard_map/ppermute | solution.py:593
  123.5 5.5 %collective-permute-start.45 = (f32[4,128]{1,0:T(4,128)S(1)}, f32[4,128]{1,0:T(4,128)S(1)}, u32[]{:S(2)}, u32[]{:S(2)}) collective-permute-start(f32[4,128]{1,0:T(4,128)S(1)} %fusion.9), channel_id=1, source_target_pairs={{0,1},{1,0},{2,3},{3,2},{4,5},{5,4},{6,7},{7,6},{8,9},{9,8},{10,11... | collective-permute-start | bytes 6152 | tf_op jit(solution)/shard_map/ppermute | solution.py:607
  125.7 11.0 %all-to-all-start.3 = ((f32[8,16,128]{2,1,0:T(8,128)}), f32[8,16,128]{2,1,0:T(8,128)S(1)}, u32[]{:S(2)}, u32[]{:S(2)}) async-start(f32[8,16,128]{2,1,0:T(8,128)} %broadcast_in_dim.8), calls=%async_computation.3 | async-start | bytes 131072 | tf_op jit(solution)/shard_map/all_to_all | solution.py:537
  129.7 29.6 %collective-permute-start.39 = (f32[128,512]{1,0:T(8,128)S(1)}, f32[128,512]{1,0:T(8,128)S(1)}, u32[]{:S(2)}, u32[]{:S(2)}) collective-permute-start(f32[128,512]{1,0:T(8,128)S(1)} %add.339), channel_id=1, source_target_pairs={{0,8},{8,16},{16,24},{24,0},{1,9},{9,17},{17,25},{25,1},{2,10},{10... | collective-permute-start | bytes 786440 | tf_op jit(solution)/shard_map/ppermute | solution.py:562
  131.6 30.3 %collective-permute-start.40 = (f32[128,512]{1,0:T(8,128)S(1)}, f32[128,512]{1,0:T(8,128)S(1)}, u32[]{:S(2)}, u32[]{:S(2)}) collective-permute-start(f32[128,512]{1,0:T(8,128)S(1)} %add.341), channel_id=1, source_target_pairs={{0,24},{8,0},{16,8},{24,16},{1,25},{9,1},{17,9},{25,17},{2,26},{10... | collective-permute-start | bytes 786440 | tf_op jit(solution)/shard_map/ppermute | solution.py:562
  132.9 22.3 %collective-permute-start.42 = (f32[128,512]{1,0:T(8,128)S(1)}, f32[128,512]{1,0:T(8,128)S(1)}, u32[]{:S(2)}, u32[]{:S(2)}) collective-permute-start(f32[128,512]{1,0:T(8,128)S(1)} %add.340), channel_id=1, source_target_pairs={{32,64},{64,32},{0,96},{96,0},{33,65},{65,33},{1,97},{97,1},{34,66... | collective-permute-start | bytes 786440 | tf_op jit(solution)/shard_map/ppermute | solution.py:561
  150.7 3.8 %collective-permute-start.46 = (f32[2,4,128]{2,1,0:T(4,128)S(1)}, f32[2,4,128]{2,1,0:T(4,128)S(1)}, u32[]{:S(2)}, u32[]{:S(2)}) collective-permute-start(f32[2,4,128]{2,1,0:T(4,128)S(1)} %dynamic-slice_bitcast_fusion), channel_id=1, source_target_pairs={{0,32},{32,0},{64,96},{96,64},{1,33},{33,1},{65,97},{97,65},{2,34}... | collective-permute-start | bytes 12296 | tf_op jit(solution)/shard_map/ppermute | solution.py:611
  150.8 7.7 %collective-permute-start.35 = (f32[136,512]{1,0:T(8,128)S(1)}, f32[136,512]{1,0:T(8,128)S(1)}, u32[]{:S(2)}, u32[]{:S(2)}) collective-permute-start(f32[136,512]{1,0:T(8,128)S(1)} %get-tuple-element.88), channel_id=1, source_target_pairs={{0,32},{32,0},{64,96},{96,64},{1,33},{33,1},{65,97},{97,65},{2,34}... | collective-permute-start | bytes 835592 | tf_op jit(solution)/shard_map/ppermute | solution.py:561
  154.5 12.8 %collective-permute-start.32 = (f32[136,512]{1,0:T(8,128)S(1)}, f32[136,512]{1,0:T(8,128)S(1)}, u32[]{:S(2)}, u32[]{:S(2)}) collective-permute-start(f32[136,512]{1,0:T(8,128)S(1)} %get-tuple-element.84), channel_id=1, source_target_pairs={{0,2},{2,4},{4,6},{6,0},{1,3},{3,5},{5,7},{7,1},{8,10},{10,12},{12... | collective-permute-start | bytes 835592 | tf_op jit(solution)/shard_map/ppermute | solution.py:562
  155.2 13.0 %collective-permute-start.33 = (f32[136,512]{1,0:T(8,128)S(1)}, f32[136,512]{1,0:T(8,128)S(1)}, u32[]{:S(2)}, u32[]{:S(2)}) collective-permute-start(f32[136,512]{1,0:T(8,128)S(1)} %get-tuple-element.85), channel_id=1, source_target_pairs={{0,6},{2,0},{4,2},{6,4},{1,7},{3,1},{5,3},{7,5},{8,14},{10,8},{12,... | collective-permute-start | bytes 835592 | tf_op jit(solution)/shard_map/ppermute | solution.py:562
  158.5 7.6 %collective-permute-start.43 = (f32[128,512]{1,0:T(8,128)S(1)}, f32[128,512]{1,0:T(8,128)S(1)}, u32[]{:S(2)}, u32[]{:S(2)}) collective-permute-start(f32[128,512]{1,0:T(8,128)S(1)} %add.353), channel_id=1, source_target_pairs={{0,8},{8,16},{16,24},{24,0},{1,9},{9,17},{17,25},{25,1},{2,10},{10... | collective-permute-start | bytes 786440 | tf_op jit(solution)/shard_map/ppermute | solution.py:563
  159.2 12.1 %collective-permute-start.38 = (f32[128,512]{1,0:T(8,128)S(1)}, f32[128,512]{1,0:T(8,128)S(1)}, u32[]{:S(2)}, u32[]{:S(2)}) collective-permute-start(f32[128,512]{1,0:T(8,128)S(1)} %add.337), channel_id=1, source_target_pairs={{0,24},{8,0},{16,8},{24,16},{1,25},{9,1},{17,9},{25,17},{2,26},{10... | collective-permute-start | bytes 786440 | tf_op jit(solution)/shard_map/ppermute | solution.py:564
  161.9 7.8 %collective-permute-start.36 = (f32[136,512]{1,0:T(8,128)S(1)}, f32[136,512]{1,0:T(8,128)S(1)}, u32[]{:S(2)}, u32[]{:S(2)}) collective-permute-start(f32[136,512]{1,0:T(8,128)S(1)} %add.346), channel_id=1, source_target_pairs={{0,2},{2,4},{4,6},{6,0},{1,3},{3,5},{5,7},{7,1},{8,10},{10,12},{12... | collective-permute-start | bytes 835592 | tf_op jit(solution)/shard_map/ppermute | solution.py:563
  166.1 10.5 %collective-permute-start.31 = (f32[136,512]{1,0:T(8,128)S(1)}, f32[136,512]{1,0:T(8,128)S(1)}, u32[]{:S(2)}, u32[]{:S(2)}) collective-permute-start(f32[136,512]{1,0:T(8,128)S(1)} %get-tuple-element.82), channel_id=1, source_target_pairs={{0,6},{2,0},{4,2},{6,4},{1,7},{3,1},{5,3},{7,5},{8,14},{10,8},{12,... | collective-permute-start | bytes 835592 | tf_op jit(solution)/shard_map/ppermute | solution.py:564
  167.3 7.7 %collective-permute-start.41 = (f32[128,512]{1,0:T(8,128)S(1)}, f32[128,512]{1,0:T(8,128)S(1)}, u32[]{:S(2)}, u32[]{:S(2)}) collective-permute-start(f32[128,512]{1,0:T(8,128)S(1)} %add_add_fusion.2), channel_id=1, source_target_pairs={{32,64},{64,32},{0,96},{96,0},{33,65},{65,33},{1,97},{97,1},{34,66... | collective-permute-start | bytes 786440 | tf_op jit(solution)/shard_map/ppermute | solution.py:565
  168.2 7.6 %collective-permute-start.44 = (f32[128,512]{1,0:T(8,128)S(1)}, f32[128,512]{1,0:T(8,128)S(1)}, u32[]{:S(2)}, u32[]{:S(2)}) collective-permute-start(f32[128,512]{1,0:T(8,128)S(1)} %add.354), channel_id=1, source_target_pairs={{0,8},{8,16},{16,24},{24,0},{1,9},{9,17},{17,25},{25,1},{2,10},{10... | collective-permute-start | bytes 786440 | tf_op jit(solution)/shard_map/ppermute | solution.py:565
  169.6 7.0 %collective-permute-start.34 = (f32[136,512]{1,0:T(8,128)S(1)}, f32[136,512]{1,0:T(8,128)S(1)}, u32[]{:S(2)}, u32[]{:S(2)}) collective-permute-start(f32[136,512]{1,0:T(8,128)S(1)} %add_add_fusion.1), channel_id=1, source_target_pairs={{0,32},{32,0},{64,96},{96,64},{1,33},{33,1},{65,97},{97,65},{2,34}... | collective-permute-start | bytes 835592 | tf_op jit(solution)/shard_map/ppermute | solution.py:565
  171.3 7.8 %collective-permute-start.37 = (f32[136,512]{1,0:T(8,128)S(1)}, f32[136,512]{1,0:T(8,128)S(1)}, u32[]{:S(2)}, u32[]{:S(2)}) collective-permute-start(f32[136,512]{1,0:T(8,128)S(1)} %add.347), channel_id=1, source_target_pairs={{0,2},{2,4},{4,6},{6,0},{1,3},{3,5},{5,7},{7,1},{8,10},{10,12},{12... | collective-permute-start | bytes 835592 | tf_op jit(solution)/shard_map/ppermute | solution.py:565
  (19 other events, 229.2 us)
